TPU v7x, 512 devices: a whole 4x4x16 slice. The times are simulated.
512 devices in a mesh: row: 32 (over z, core), col: 16 (over y, x).
Axes of the slice: x: 4, y: 4, z: 16, core: 2. Of those that a mesh axis runs over, the one named last changes fastest.
Arguments:
- gbar: float32 [4, 4096, 8, 2048], P(None, 'row', None, 'col'), as said below
- panel: float32 [8, 2048, 256], P(None, ('col', 'row')), may hold values from -0.046875 to 0.046875
- panel_adj: float32 [4, 4096, 256], P(None, ('row', 'col')), may hold values from -6 to 6
- factor: float32 [256, 256], replicated, as said below
- factor_adj: float32 [256, 256], replicated, may hold values from -6 to 6
Outputs:
- lower_adj: float32 [4, 4096, 256], P(None, ('row', 'col'))
- corner_adj: float32 [256, 256], replicated
Inputs may be any that keep to these rules, and one draw needn't show every extreme that they name: gbar holds a symmetric 16384 x 16384 matrix. factor is lower triangular with a positive diagonal.
All inputs are finite; a program needn't handle non-finite values.
Results may differ from a plain program's by a relative error of at most 0.000075.
Values sent between devices are 32-bit elements; how exact they have to be, the bound alone decides.
No kernel may reach another device: no remote copies, remote signals or barrier semaphores. Data moves between devices by JAX's collectives and lax.ppermute only.
A program may use at most 64 MiB of HBM per device.

v0:
```python
import jax
import jax.numpy as jnp
from jax import lax
from jax.sharding import PartitionSpec as P


def broadcast(value, axis, source):
    kept = jnp.where(lax.axis_index(axis) == source, value, 0).astype(value.dtype)
    return lax.psum(kept, axis)


def corner_reduce(corner):
    return lax.psum(corner, ("row", "col"))


def per_device(gbar, panel, panel_adj, factor, factor_adj):
    highest = lax.Precision.HIGHEST
    row_at = lax.axis_index("row")
    col_at = lax.axis_index("col")
    n_row = lax.axis_size("row")
    n_col = lax.axis_size("col")
    panel_width = factor.shape[0]
    row_share = panel_adj.shape[1]
    column = lax.all_gather(panel, "row", axis=1, tiled=True)
    product = jnp.einsum(
        "arcs,csk->ark", gbar, column, precision=highest, preferred_element_type=jnp.float32
    )
    spread = jnp.zeros(product.shape, jnp.float32)
    spread = lax.dynamic_update_slice_in_dim(spread, panel_adj, col_at * row_share, 1)
    partial_value = spread - 2.0 * product
    inverse = jax.scipy.linalg.solve_triangular(
        factor, jnp.eye(panel_width, dtype=jnp.float32), lower=True
    )
    stride_ratio = n_row // n_col
    blocks = column.shape[0] // stride_ratio
    local_rows = lax.dynamic_index_in_dim(
        column.reshape(blocks, stride_ratio, column.shape[1], panel_width),
        row_at // n_col,
        1,
        keepdims=False,
    )
    rows_here = broadcast(local_rows, "col", row_at % n_col)
    mine = lax.dynamic_slice_in_dim(rows_here, col_at * row_share, row_share, 1)
    summed = lax.psum(partial_value, "col")
    owned_part = lax.dynamic_slice_in_dim(summed, col_at * row_share, row_share, 1)
    owned_rows = jnp.einsum(
        "ark,kj->arj", owned_part, inverse, precision=highest, preferred_element_type=jnp.float32
    )
    corner = jnp.einsum(
        "ark,arj->kj", owned_rows, mine, precision=highest, preferred_element_type=jnp.float32
    )
    corner_total = corner_reduce(corner)
    adjusted = factor_adj - corner_total
    projected = jnp.dot(factor.T, adjusted, precision=highest, preferred_element_type=jnp.float32)
    halved = jnp.tril(projected) - 0.5 * jnp.diag(jnp.diag(projected))
    middle = jnp.dot(
        jnp.dot(inverse.T, halved, precision=highest, preferred_element_type=jnp.float32),
        inverse,
        precision=highest,
        preferred_element_type=jnp.float32,
    )
    return (owned_rows, 0.5 * (middle + middle.T))


def solution(mesh):
    return jax.shard_map(
        per_device,
        mesh=mesh,
        in_specs=(
            P(None, "row", None, "col"),
            P(None, ("col", "row"), None),
            P(None, ("row", "col"), None),
            P(),
            P(),
        ),
        out_specs=(P(None, ("row", "col"), None), P()),
        check_vma=False,
    )
```

profile of v0, /device:TPU:1, one launch (start us, length us, event | category | flops | bytes accessed | tf_op | source)
XLA Modules:
  0.0 682.6 jit_solution(6590881402351927959)
XLA Ops:
  7.2 0.0 all-gather.2.cloned.1.call-start
  7.2 1.4 copy.21
  8.6 0.0 all-gather.2.cloned.1.call-update
  8.6 0.0 all-reduce.6.cloned.1.call-start
  8.7 0.0 copy-start.4
  8.7 0.0 copy-start.1
  8.7 2.1 copy.22
  10.9 0.0 copy-done.4
  10.9 0.0 copy-done.1
  11.0 76.1 %all-gather.2.cloned.1.call-done = f32[8,128,256]{2,0,1:T(8,128)} async-done(((f32[8,4,256]{2,0,1:T(8,128)}), f32[8,128,256]{2,0,1:T(8,128)}) %all-gather.2.cloned.1.call-update) | async-done | bytes 1048592 | tf_op jit(solution)/shard_map/all_gather | solution.py:24
  87.1 0.0 copy-start
  87.1 1.7 copy.23
  88.7 0.9 fusion.3
  89.6 0.0 copy-done
  89.6 4.3 fusion.1
  93.9 0.0 copy-start.2
  93.9 0.0 all-reduce.6.cloned.1.call-update
  93.9 0.0 all-reduce.4.cloned.1.call-start
  94.0 0.1 triangular_solve.68
  94.0 3.8 while.1
  94.0 0.6 fusion.39
  94.6 1.3 bitcast_dynamic-update-slice_fusion.2
  95.9 0.6 fusion.39
  96.5 1.3 bitcast_dynamic-update-slice_fusion.2
  97.8 19.7 %custom-call.4 = f32[2,128,128]{1,2,0:T(8,128)S(1)} custom-call(f32[2,128,128]{2,1,0:T(8,128)S(1)} %get-tuple-element.9), custom_call_target="InvertDiagBlocksLowerTriangular" | custom-call | tf_op jit(solution)/shard_map/jit(_solve_triangular)/triangular_solve | solution.py:31
  117.5 0.3 fusion.18
  117.8 0.3 convolution_subtract_fusion
  118.1 0.3 fusion.21
  118.4 88.9 %all-reduce.6.cloned.1.call-done = (f32[4,128,256]{2,1,0:T(8,128)}, f32[4,128,256]{2,1,0:T(8,128)}) async-done(((f32[4,128,256]{2,1,0:T(8,128)}, f32[4,128,256]{2,1,0:T(8,128)}), (f32[4,128,256]{2,1,0:T(8,128)}, f32[4,128,256]{2,1,0:T(8,128)})) %all-reduce.6.cloned.1.call-update) | async-done | bytes 1048592 | tf_op jit(solution)/shard_map/psum | solution.py:44
  207.3 1.0 fusion.5
  208.3 0.0 copy-start.3
  208.3 1.9 convolution_bitcast_fusion.2
  210.2 0.0 all-reduce.4.cloned.1.call-update
  210.2 460.0 %all-reduce.4.cloned.1.call-done = f32[256,256]{1,0:T(8,128)} async-done(((f32[256,256]{1,0:T(8,128)}), f32[256,256]{1,0:T(8,128)}) %all-reduce.4.cloned.1.call-update) | async-done | bytes 262160 | tf_op jit(solution)/shard_map/psum | solution.py:13
  670.2 0.0 copy-done.2
  670.2 1.5 convolution_bitcast_fusion.1
  671.8 2.3 gather_fusion
  674.1 0.7 fusion.7
  674.8 0.4 fusion.14
  675.2 0.0 copy-done.3
  675.2 0.1 copy.26
  675.3 0.7 fusion.4
  (9 shorter events, 0.1 us)
Async XLA Ops:
  7.2 79.9 %all-gather.2.cloned.1.call-start = ((), (), s32[]{:S(2)}) async-start(), calls=%async_computation | async-start | bytes 1081344 | tf_op jit(solution)/shard_map/all_gather | solution.py:24
  8.6 198.6 %all-reduce.6.cloned.1.call-start = ((), (), s32[]{:S(2)}) async-start(), calls=%async_computation.2 | async-start | bytes 2097152 | tf_op jit(solution)/shard_map/psum | solution.py:44
  8.7 2.2 copy-start.4
  8.7 2.2 copy-start.1
  87.1 2.5 copy-start
  93.9 576.4 %copy-start.2 = (f32[256,256]{1,0:T(8,128)S(1)}, f32[256,256]{1,0:T(8,128)}, u32[]{:S(2)}) copy-start(f32[256,256]{1,0:T(8,128)} %param.9) | copy-start | bytes 786436
  93.9 576.3 %all-reduce.4.cloned.1.call-start = ((), (), s32[]{:S(2)}) async-start(), calls=%async_computation.1 | async-start | bytes 524288 | tf_op jit(solution)/shard_map/psum | solution.py:13
  208.3 466.9 %copy-start.3 = (f32[4,8,256]{2,1,0:T(8,128)}, f32[4,8,256]{2,1,0:T(8,128)S(1)}, u32[]{:S(2)}) copy-start(f32[4,8,256]{2,1,0:T(8,128)S(1)} %fusion.5) | copy-start | bytes 98308
Sparse Core Ops, SparseCore 0:
  10.7 76.3 all-gather.1
  94.0 113.1 all-reduce.5
  213.3 456.8 all-reduce.3
where the time goes:
time: 684 us; the launch traced here: 683 us
  waiting for transfers between devices  625 us (91%)
  other arithmetic  21.3 us (3%)
  between operations  14 us (2%)
  local copies, waits for them, and re-layouts  11.5 us (2%)
  matrix products  10.6 us (2%)
    psum x1, waiting for transfers between devices, corner_reduce(): return lax.psum(corner, ('row', 'col'))  460 us
    psum x1, waiting for transfers between devices, per_device(): summed = lax.psum(partial_value, 'col')  88.9 us
    all_gather x1, waiting for transfers between devices, per_device(): column = lax.all_gather(panel, 'row', axis=1, tiled=True)  76.1 us
    another operation x3, other arithmetic, per_device(): jax.scipy.linalg.solve_triangular(factor, jnp.eye(panel_width, dtype=jnp....  19.7 us
  transfers between devices with their start and end apart: 3, of which 3 were waited for; matrix products, arithmetic and copies ran while one was open for 4% of the time, Pallas kernels for 0%

commit v1 on v0

v1 whole, which is shorter than its diff:
```python
import jax
import jax.numpy as jnp
from jax import lax
from jax.sharding import Mesh
from jax.sharding import PartitionSpec as P


def dot(a, b):
    return jnp.dot(a, b, precision=lax.Precision.HIGHEST, preferred_element_type=jnp.float32)


def spread(block, axis):
    n = lax.axis_size(axis)
    return lax.all_to_all(jnp.broadcast_to(block[None], (n,) + block.shape), axis, 0, 0, tiled=True)


def per_device(gbar, panel, panel_adj, factor, factor_adj):
    highest = lax.Precision.HIGHEST
    core_at = lax.axis_index("core")
    row_at = lax.axis_index("z") * lax.axis_size("core") + core_at
    col_at = lax.axis_index("col")
    n_z = lax.axis_size("z")
    n_core = lax.axis_size("core")
    n_col = lax.axis_size("col")
    width = factor.shape[0]
    row_blocks, rows, col_blocks, cols = gbar.shape
    share = panel_adj.shape[1]
    part = panel.shape[1]
    own = panel.reshape(col_blocks * part, width)
    along_z = lax.all_gather(own, "z", axis=0)
    both = lax.all_gather(along_z, "core", axis=0)
    column = both.reshape(n_core, n_z, col_blocks, part, width).transpose(2, 1, 0, 3, 4)
    column = column.reshape(col_blocks, cols, width)
    product = jnp.einsum(
        "arcs,csk->ark", gbar, column, precision=highest, preferred_element_type=jnp.float32
    )
    inverse = jax.scipy.linalg.solve_triangular(
        factor, jnp.eye(width, dtype=jnp.float32), lower=True
    )
    ratio = col_blocks // row_blocks
    local = lax.dynamic_index_in_dim(
        column.reshape(row_blocks, ratio, cols, width), row_at // n_col, 1, keepdims=False
    )
    sent = jnp.stack([product, local])
    sent = sent.reshape(2, row_blocks, n_col, share, width).transpose(2, 0, 1, 3, 4)
    got = lax.all_to_all(sent, "col", 0, 0, tiled=True)
    total = panel_adj - 2.0 * jnp.sum(got[:, 0], axis=0)
    mine = lax.dynamic_index_in_dim(got[:, 1], row_at % n_col, 0, keepdims=False)
    total = total.reshape(row_blocks * share, width)
    mine = mine.reshape(row_blocks * share, width)
    lower = dot(total, inverse)
    corner = dot(mine.T, lower)
    slices = lax.all_to_all(corner.reshape(n_col, width // n_col, width), "col", 0, 0, tiled=True)
    slice_col = jnp.sum(slices, axis=0)
    half = width // n_col // n_core
    halves = lax.all_to_all(slice_col.reshape(n_core, half, width), "core", 0, 0, tiled=True)
    piece = jnp.sum(halves, axis=0)
    piece = jnp.sum(spread(piece, "z"), axis=0)
    begin = (col_at * n_core + core_at) * half
    adjusted = lax.dynamic_slice_in_dim(factor_adj.T, begin, half, 0) - piece
    projected = dot(adjusted, factor)
    at_row = begin + lax.broadcasted_iota(jnp.int32, projected.shape, 0)
    at_col = lax.broadcasted_iota(jnp.int32, projected.shape, 1)
    scale = jnp.where(at_row < at_col, 1.0, jnp.where(at_row == at_col, 0.5, 0.0))
    halved = jnp.where(at_row <= at_col, projected * scale, 0.0)
    stage = dot(halved, inverse)
    stage = lax.all_gather(stage, "core", axis=0, tiled=True)
    stage = spread(stage, "col").reshape(width, width)
    middle = dot(inverse.T, stage)
    return (lower.reshape(row_blocks, share, width), 0.5 * (middle + middle.T))


def solution(mesh):
    devices = mesh.devices
    wide = Mesh(devices.reshape(devices.shape[0] // 2, 2, devices.shape[1]), ("z", "core", "col"))
    row = ("z", "core")
    return jax.shard_map(
        per_device,
        mesh=wide,
        in_specs=(
            P(None, row, None, "col"),
            P(None, ("col",) + row, None),
            P(None, row + ("col",), None),
            P(),
            P(),
        ),
        out_specs=(P(None, row + ("col",), None), P()),
        check_vma=False,
    )
```

time: 684 us -> 173 us (0.25)
  waiting for transfers between devices: 625 us -> 35.5 us
  blocking collectives: 0 us -> 66.9 us
  starting transfers between devices: 0.12 us -> 17.6 us
    psum x2 -> x0, waiting for transfers between devices: 549 us -> none  [the longest x1 460 us: corner_reduce(): return lax.psum(corner, ('row', 'col'))]
    all_gather x1, waiting for transfers between devices: 76.1 us -> 23.6 us  [per_device(): both = lax.all_gather(along_z, 'core', axis=0)]
    all_gather x0 -> x2, blocking collectives: none -> 36.6 us  [the longest x1 31.8 us: per_device(): along_z = lax.all_gather(own, 'z', axis=0)]
    all_to_all x0 -> x3, blocking collectives: none -> 30.4 us  [the longest x1 14 us: per_device(): lax.all_to_all(corner.reshape(n_col, width // n_col, width), 'col', 0, 0,...]
    all_to_all x0 -> x2, starting transfers between devices: none -> 17.5 us  [the longest x1 12 us: spread(): lax.all_to_all(jnp.broadcast_to(block[None], (n,) + block.shape), axis, 0...]
    all_to_all x0 -> x2, waiting for transfers between devices: none -> 12 us  [the longest x1 11.9 us: spread(): lax.all_to_all(jnp.broadcast_to(block[None], (n,) + block.shape), axis, 0...]
  transfers between devices with their start and end apart: 3 -> 3, of which waited for: 3 -> 2; matrix products, arithmetic and copies ran while one was open for 4% -> 15% of each run, Pallas kernels for 0% -> 0%
where the time goes in v1:
time: 173 us
  blocking collectives  66.9 us (39%)
  waiting for transfers between devices  35.5 us (21%)
  other arithmetic  21.4 us (12%)
  starting transfers between devices  17.6 us (10%)
  between operations  14.4 us (8%)
  local copies, waits for them, and re-layouts  10.9 us (6%)
  matrix products  5.92 us (3%)
    all_gather x1, blocking collectives, per_device(): along_z = lax.all_gather(own, 'z', axis=0)  31.8 us
    all_gather x1, waiting for transfers between devices, per_device(): both = lax.all_gather(along_z, 'core', axis=0)  23.6 us
    another operation x3, other arithmetic, per_device(): jax.scipy.linalg.solve_triangular(factor, jnp.eye(width, dtype=jnp.float3...  20.4 us
    all_to_all x1, blocking collectives, per_device(): lax.all_to_all(corner.reshape(n_col, width // n_col, width), 'col', 0, 0,...  14 us
    all_to_all x1, starting transfers between devices, spread(): lax.all_to_all(jnp.broadcast_to(block[None], (n,) + block.shape), axis, 0...  12 us
    all_to_all x1, waiting for transfers between devices, spread(): lax.all_to_all(jnp.broadcast_to(block[None], (n,) + block.shape), axis, 0...  11.9 us
    all_to_all x1, blocking collectives, spread(): lax.all_to_all(jnp.broadcast_to(block[None], (n,) + block.shape), axis, 0...  10.8 us
    all_to_all x1, blocking collectives, per_device(): lax.all_to_all(slice_col.reshape(n_core, half, width), 'core', 0, 0, tile...  5.57 us
  transfers between devices with their start and end apart: 3, of which 2 were waited for; matrix products, arithmetic and copies ran while one was open for 15% of the time, Pallas kernels for 0%

profile of v1, /device:TPU:1, one launch (start us, length us, event | category | flops | bytes accessed | tf_op | source)
XLA Modules:
  0.0 172.7 jit_solution(13303605667777561292)
XLA Ops:
  7.2 0.0 copy-start
  7.2 0.0 copy-start.2
  7.2 0.0 all-gather.3.cloned.1.call-start
  7.2 0.8 all_gather_reshape.3
  8.1 31.8 %all_gather.12 = f32[16,32,256]{2,1,0:T(8,128)S(1)} all-gather(f32[1,32,256]{2,1,0:T(8,128)S(1)} %all_gather_reshape.3), channel_id=1, replica_groups=mesh['z'=16,'core'=2,'col'=16] {'z'}, dimensions={0}, use_global_device_ids=true | all-gather | bytes 557056 | tf_op jit(solution)/shard_map/all_gather | solution.py:30
  39.9 1.1 copy.26
  41.0 0.0 all-gather.3.cloned.1.call-update
  41.1 0.0 copy-done.2
  41.1 0.7 fusion.8
  41.8 23.6 %all-gather.3.cloned.1.call-done = f32[32,32,256]{2,0,1:T(8,128)} async-done(((f32[16,32,256]{2,0,1:T(8,128)}), f32[32,32,256]{2,0,1:T(8,128)}) %all-gather.3.cloned.1.call-update) | async-done | bytes 1048592 | tf_op jit(solution)/shard_map/all_gather | solution.py:31
  65.4 1.9 %copy.27 = f32[8,16,2,4,256]{4,3,2,1,0:T(4,128)S(1)} copy(f32[8,16,2,4,256]{4,1,2,3,0:T(8,128)} %bitcast.60) | data formatting | bytes 2097152 | tf_op jit(solution)/shard_map/transpose | solution.py:32
  67.3 0.4 reshape_reshape.3
  67.6 0.4 reshape.79
  68.0 3.5 %fusion.2 = f32[1,4,16,8,256]{4,3,2,1,0:T(8,128)S(1)} fusion(f32[4,16,8,8,128]{4,3,2,1,0:T(8,128)} %bitcast.58, f32[8,128,256,1,1]{2,1,0,3,4:T(8,128)S(1)} %reshape.79), kind=kOutput, calls=%fused_computation.4 | convolution fusion | flops 1610612736 | bytes 3670016 | tf_op jit(solution)/shard_map/arcs,csk->ark/dot_general | solution.py:34
  71.6 0.1 maximum_bitcast_fusion
  71.7 0.0 copy-start.1
  71.7 1.1 copy.30
  72.8 5.5 %all-to-all-start = ((f32[16,2,4,8,256]{4,3,2,1,0:T(8,128)}), f32[16,2,4,8,256]{4,3,2,1,0:T(8,128)S(1)}, u32[]{:S(2)}, u32[]{:S(2)}) async-start(f32[16,2,4,8,256]{4,3,2,1,0:T(8,128)} %copy.30), calls=%async_computation | async-start | bytes 2097152 | tf_op jit(solution)/shard_map/all_to_all | solution.py:46
  78.3 0.0 copy-start.5
  78.3 0.1 triangular_solve.60
  78.4 0.0 copy-done.1
  78.4 4.1 %while.1 = (s32[]{:T(128)}, f32[256,256]{1,0:T(8,128)S(1)}, s32[2,2]{1,0:T(2,128)S(1)}, f32[2,128,128]{2,1,0:T(8,128)S(1)}, s32[]{:T(128)}) while((s32[]{:T(128)}, f32[256,256]{1,0:T(8,128)S(1)}, s32[2,2]{1,0:T(2,128)S(1)}, f32[2,128,128]{2,1,0:T(8,128)S(1)}, s32[]{:T(128)}) %tuple.29), condition=%wide.while_cond, body=%wide.while_body.sunk | while | flops 2 | bytes 131181 | solution.py:37
  78.4 0.6 fusion.35
  79.0 1.4 bitcast_dynamic-update-slice_fusion.2
  80.5 0.6 fusion.35
  81.0 1.4 bitcast_dynamic-update-slice_fusion.2
  82.5 19.7 %custom-call.4 = f32[2,128,128]{1,2,0:T(8,128)S(1)} custom-call(f32[2,128,128]{2,1,0:T(8,128)S(1)} %get-tuple-element.9), custom_call_target="InvertDiagBlocksLowerTriangular" | custom-call | tf_op jit(solution)/shard_map/jit(_solve_triangular)/triangular_solve | solution.py:37
  102.2 0.3 fusion.12
  102.5 0.3 convolution_subtract_fusion
  102.8 0.3 fusion.15
  103.1 0.0 copy-start.3
  103.1 0.0 all-to-all-done
  103.1 0.1 fusion.27
  103.2 0.1 copy.32
  103.3 0.0 copy-done.5
  103.3 0.2 fusion.11
  103.5 0.0 copy-start.4
  103.6 0.3 fusion.16
  103.9 14.0 %all_to_all.25 = f32[16,16,256]{2,1,0:T(8,128)S(1)} all-to-all(f32[16,16,256]{2,1,0:T(8,128)S(1)} %fusion.16), channel_id=1, replica_groups=mesh['z'=16,'core'=2,'col'=16] {'col'}, dimensions={0} | all-to-all | bytes 524288 | tf_op jit(solution)/shard_map/all_to_all | solution.py:53
  117.9 5.6 %all_to_all.26 = f32[2,8,256]{2,1,0:T(8,128)S(1)} all-to-all(f32[2,8,256]{2,1,0:T(8,128)S(1)} %bitcast.63), channel_id=1, replica_groups=mesh['z'=16,'core'=2,'col'=16] {'core'}, dimensions={0} | all-to-all | bytes 32768 | tf_op jit(solution)/shard_map/all_to_all | solution.py:56
  123.5 0.7 broadcast_in_dim.26
  124.2 12.0 %all-to-all-start.3 = ((f32[16,8,256]{2,1,0:T(8,128)}), f32[16,8,256]{2,1,0:T(8,128)S(1)}, u32[]{:S(2)}, u32[]{:S(2)}) async-start(f32[16,8,256]{2,1,0:T(8,128)} %broadcast_in_dim.26), calls=%async_computation.3 | async-start | bytes 262144 | tf_op jit(solution)/shard_map/all_to_all | solution.py:14
  136.2 0.0 copy-done
  136.2 0.1 constant_dynamic-slice_fusion.1
  136.3 0.1 copy.36
  136.4 11.9 %all-to-all-done.3 = f32[16,8,256]{2,1,0:T(8,128)S(1)} async-done(((f32[16,8,256]{2,1,0:T(8,128)}), f32[16,8,256]{2,1,0:T(8,128)S(1)}, u32[]{:S(2)}, u32[]{:S(2)}) %all-to-all-start.3) | async-done | bytes 131104 | tf_op jit(solution)/shard_map/all_to_all | solution.py:14
  148.4 0.0 copy-done.3
  148.4 0.2 fusion.5
  148.6 0.2 fusion.10
  148.8 4.8 %all_gather.15 = f32[16,256]{1,0:T(8,128)S(1)} all-gather(f32[8,256]{1,0:T(8,128)S(1)} %fusion.10), channel_id=1, replica_groups=mesh['z'=16,'core'=2,'col'=16] {'core'}, dimensions={0}, use_global_device_ids=true | all-gather | bytes 24576 | tf_op jit(solution)/shard_map/all_gather | solution.py:67
  153.6 10.8 %all_to_all.27 = f32[16,16,256]{2,1,0:T(8,128)S(1)} all-to-all(f32[16,16,256]{2,1,0:T(8,128)S(1)} %broadcast_in_dim.30), channel_id=1, replica_groups=mesh['z'=16,'core'=2,'col'=16] {'col'}, dimensions={0} | all-to-all | bytes 524288 | tf_op jit(solution)/shard_map/all_to_all | solution.py:14
  164.4 0.6 fusion.9
  165.0 0.0 copy-done.4
  165.0 0.1 copy.33
  165.1 0.7 fusion.7
  (12 shorter events, 0.2 us)
Async XLA Ops:
  7.2 129.0 %copy-start = (f32[256,256]{1,0:T(8,128)S(1)}, f32[256,256]{1,0:T(8,128)}, u32[]{:S(2)}) copy-start(f32[256,256]{1,0:T(8,128)} %param.9) | copy-start | bytes 786436
  7.2 33.9 %copy-start.2 = (f32[256,256]{1,0:T(8,128)S(1)}, f32[256,256]{1,0:T(8,128)}, u32[]{:S(2)}) copy-start(f32[256,256]{1,0:T(8,128)} %param.8) | copy-start | bytes 786436
  7.2 58.2 %all-gather.3.cloned.1.call-start = ((), (), s32[]{:S(2)}) async-start(), calls=%async_computation.5 | async-start | bytes 1572864 | tf_op jit(solution)/shard_map/all_gather | solution.py:31
  71.7 6.7 %copy-start.1 = (f32[256,256]{1,0:T(8,128)S(1)}, f32[256,256]{1,0:T(8,128)}, u32[]{:S(2)}) copy-start(f32[256,256]{1,0:T(8,128)} %fusion.8) | copy-start | bytes 786436
  72.8 30.3 %all-to-all-start = ((f32[16,2,4,8,256]{4,3,2,1,0:T(8,128)}), f32[16,2,4,8,256]{4,3,2,1,0:T(8,128)S(1)}, u32[]{:S(2)}, u32[]{:S(2)}) async-start(f32[16,2,4,8,256]{4,3,2,1,0:T(8,128)} %copy.30), calls=%async_computation | async-start | bytes 2097152 | tf_op jit(solution)/shard_map/all_to_all | solution.py:46
  78.3 25.0 %copy-start.5 = (f32[4,8,256]{2,1,0:T(8,128)S(1)}, f32[4,8,256]{2,1,0:T(8,128)}, u32[]{:S(2)}) copy-start(f32[4,8,256]{2,1,0:T(8,128)} %param.7) | copy-start | bytes 98308
  103.1 45.3 %copy-start.3 = (f32[256,256]{1,0:T(8,128)S(1)}, f32[256,256]{1,0:T(8,128)}, u32[]{:S(2)}) copy-start(f32[256,256]{1,0:T(8,128)} %param.8) | copy-start | bytes 786436
  103.5 61.4 %copy-start.4 = (f32[32,256]{1,0:T(8,128)}, f32[32,256]{1,0:T(8,128)S(1)}, u32[]{:S(2)}) copy-start(f32[32,256]{1,0:T(8,128)S(1)} %fusion.11) | copy-start | bytes 98308
  124.2 24.2 %all-to-all-start.3 = ((f32[16,8,256]{2,1,0:T(8,128)}), f32[16,8,256]{2,1,0:T(8,128)S(1)}, u32[]{:S(2)}, u32[]{:S(2)}) async-start(f32[16,8,256]{2,1,0:T(8,128)} %broadcast_in_dim.26), calls=%async_computation.3 | async-start | bytes 262144 | tf_op jit(solution)/shard_map/all_to_all | solution.py:14
Sparse Core Ops, SparseCore 0:
  41.1 24.1 all-gather.2

commit v2 on v1

v2 whole, which is shorter than its diff:
```python
import jax
import jax.numpy as jnp
from jax import lax
from jax.experimental import pallas as pl
from jax.experimental.pallas import tpu as pltpu
from jax.sharding import Mesh
from jax.sharding import PartitionSpec as P

HIGHEST = lax.Precision.HIGHEST
F32 = jnp.float32


def dot(a, b):
    return jnp.dot(a, b, precision=HIGHEST, preferred_element_type=F32)


def dot_tn(a, b):
    return lax.dot_general(
        a, b, (((0,), (0,)), ((), ())), precision=HIGHEST, preferred_element_type=F32
    )


def call(kernel, outs, *args, scratch=(), scalars=0, cost=None):
    specs = [pl.BlockSpec(memory_space=pltpu.SMEM)] * scalars
    specs += [pl.BlockSpec(memory_space=pltpu.VMEM)] * (len(args) - scalars)
    return pl.pallas_call(
        kernel,
        out_shape=jax.tree.map(lambda s: jax.ShapeDtypeStruct(s, F32), outs, is_leaf=lambda s: isinstance(s, tuple) and isinstance(s[0], int)),
        in_specs=specs,
        scratch_shapes=scratch,
        cost_estimate=cost,
        compiler_params=pltpu.CompilerParams(vmem_limit_bytes=32 << 20),
    )(*args)


def invert_kernel(factor_ref, out_ref):
    n = factor_ref.shape[0]
    i = lax.broadcasted_iota(jnp.int32, (n, n), 0)
    j = lax.broadcasted_iota(jnp.int32, (n, n), 1)
    lower = factor_ref[...]
    out_ref[...] = jnp.where(i == j, 1.0 / jnp.where(i == j, lower, 1.0), 0.0)
    size = 1
    while size < n:
        below = (i // size == j // size + 1) & (j // size % 2 == 0)
        now = out_ref[...]
        out_ref[...] = now - dot(dot(now, jnp.where(below, lower, 0.0)), now)
        size *= 2


def product_kernel(parity_ref, gbar_ref, both_ref, out_ref, column_ref):
    n_core, n_z, depth, width = both_ref.shape
    col_blocks = column_ref.shape[0]
    row_blocks = gbar_ref.shape[0]
    part = depth // col_blocks
    cols = gbar_ref.shape[2]
    rows = gbar_ref.shape[1] // col_blocks
    share = out_ref.shape[2] // row_blocks
    n_col = out_ref.shape[0]
    for c in range(col_blocks):
        for core in range(n_core):
            column_ref[c, :, core * part:(core + 1) * part, :] = both_ref[core, :, c * part:(c + 1) * part, :]
    full = column_ref[...].reshape(col_blocks * cols, width)
    for b in range(row_blocks):
        left = jnp.concatenate(
            [gbar_ref[b, pl.ds(c, rows, stride=col_blocks), :] for c in range(col_blocks)], axis=1
        )
        out_ref[:, 0, b * share:(b + 1) * share, :] = dot(left, full).reshape(n_col, share, width)
    ratio = col_blocks // row_blocks
    for b in range(row_blocks):
        local = column_ref[b * ratio + parity_ref[0]]
        out_ref[:, 1, b * share:(b + 1) * share, :] = local.reshape(n_col, share, width)


def owned_kernel(source_ref, got_ref, adjoint_ref, inverse_ref, lower_ref, corner_ref):
    n_col = got_ref.shape[0]
    total = got_ref[0, 0]
    for c in range(1, n_col):
        total = total + got_ref[c, 0]
    lower = dot(adjoint_ref[...] - 2.0 * total, inverse_ref[...])
    lower_ref[...] = lower
    corner_ref[...] = dot_tn(got_ref[source_ref[0], 1], lower).reshape(corner_ref.shape)


def fold_kernel(parts_ref, out_ref):
    total = jnp.sum(parts_ref[...], axis=0)
    out_ref[...] = jnp.broadcast_to(total[None], out_ref.shape)


def slice_kernel(begin_ref, parts_ref, adjoint_ref, factor_ref, inverse_ref, out_ref):
    count = out_ref.shape[1]
    begin = pl.multiple_of(begin_ref[0], count)
    adjusted = adjoint_ref[pl.ds(begin, count), :] - jnp.sum(parts_ref[...], axis=0)
    projected = dot(adjusted, factor_ref[...])
    at_row = begin + lax.broadcasted_iota(jnp.int32, projected.shape, 0)
    at_col = lax.broadcasted_iota(jnp.int32, projected.shape, 1)
    halved = jnp.where(at_row < at_col, projected, jnp.where(at_row == at_col, 0.5 * projected, 0.0))
    stage = dot(halved, inverse_ref[...])
    out_ref[...] = jnp.broadcast_to(stage[None], out_ref.shape)


def finish_kernel(stage_ref, inverse_ref, out_ref):
    middle = dot_tn(inverse_ref[...], stage_ref[...])
    out_ref[...] = 0.5 * (middle + middle.T)


def per_device(gbar, panel, panel_adj, factor, factor_adj):
    n_z, n_core, n_col = (lax.axis_size(a) for a in ("z", "core", "col"))
    core_at = lax.axis_index("core")
    col_at = lax.axis_index("col")
    row_at = lax.axis_index("z") * n_core + core_at
    width = factor.shape[0]
    row_blocks, rows, col_blocks, cols = gbar.shape
    share = panel_adj.shape[1]
    part = panel.shape[1]
    near = ("core", "col")
    n_near = n_core * n_col
    count = width // n_near
    own = panel.reshape(col_blocks * part, width)
    along_z = lax.all_gather(own, "z", axis=0)
    both = lax.all_to_all(
        jnp.broadcast_to(along_z[None], (n_core,) + along_z.shape), "core", 0, 0, tiled=True
    )
    sent = call(
        product_kernel,
        (n_col, 2, row_blocks * share, width),
        (row_at // n_col)[None],
        gbar.reshape(row_blocks, rows * col_blocks, cols),
        both,
        scratch=[pltpu.VMEM((col_blocks, n_z, n_core * part, width), F32)],
        scalars=1,
        cost=pl.CostEstimate(flops=int(1.6e9), bytes_accessed=4 << 20, transcendentals=0),
    )
    got = lax.all_to_all(sent, "col", 0, 0, tiled=True)
    inverse = call(
        invert_kernel,
        (width, width),
        factor,
        cost=pl.CostEstimate(flops=int(3.2e9), bytes_accessed=1 << 19, transcendentals=0),
    )
    lower, corner = call(
        owned_kernel,
        [(row_blocks * share, width), (n_near, count, width)],
        (row_at % n_col)[None],
        got,
        panel_adj.reshape(row_blocks * share, width),
        inverse,
        scalars=1,
    )
    slices = lax.all_to_all(corner, near, 0, 0, tiled=True)
    piece = lax.all_to_all(call(fold_kernel, (n_z, count, width), slices), "z", 0, 0, tiled=True)
    stage = call(
        slice_kernel,
        (n_near, count, width),
        ((core_at * n_col + col_at) * count)[None],
        piece,
        factor_adj.T,
        factor,
        inverse,
        scalars=1,
    )
    stage = lax.all_to_all(stage, near, 0, 0, tiled=True).reshape(width, width)
    corner_adj = call(finish_kernel, (width, width), stage, inverse)
    return lower.reshape(row_blocks, share, width), corner_adj


def solution(mesh):
    devices = mesh.devices
    wide = Mesh(devices.reshape(devices.shape[0] // 2, 2, devices.shape[1]), ("z", "core", "col"))
    row = ("z", "core")
    return jax.shard_map(
        per_device,
        mesh=wide,
        in_specs=(
            P(None, row, None, "col"),
            P(None, ("col",) + row, None),
            P(None, row + ("col",), None),
            P(),
            P(),
        ),
        out_specs=(P(None, row + ("col",), None), P()),
        check_vma=False,
    )
```

time: 173 us -> 125 us (0.72)
  other arithmetic: 21.4 us -> 0 us
  Pallas kernels: 0 us -> 14.3 us
  between operations: 14.4 us -> 0.73 us
  waiting for transfers between devices: 35.5 us -> 22.2 us
  local copies, waits for them, and re-layouts: 10.9 us -> 2.02 us
  starting transfers between devices: 17.6 us -> 24.8 us
  blocking collectives: 66.9 us -> 60.8 us
  matrix products: 5.92 us -> 0 us
    all_gather x1 -> x0, waiting for transfers between devices: 23.6 us -> none  [per_device(): both = lax.all_gather(along_z, 'core', axis=0)]
    another operation x3 -> x0, other arithmetic: 20.4 us -> none  [per_device(): jax.scipy.linalg.solve_triangular(factor, jnp.eye(width, dtype=jnp.float3...]
    pallas_call x0 -> x6, Pallas kernels: none -> 14.3 us  [call(): pl.pallas_call(kernel, out_shape=jax.tree.map(lambda s: jax.ShapeDtypeStr...]
    all_to_all x1, waiting for transfers between devices: 0.01 us -> 8.67 us  [per_device(): got = lax.all_to_all(sent, 'col', 0, 0, tiled=True)]
    all_to_all x1 -> x2, starting transfers between devices: 12 us -> 17.9 us  [the longest x1 11.8 us: per_device(): lax.all_to_all(jnp.broadcast_to(along_z[None], (n_core,) + along_z.shape)...]
    dot_general x6 -> x0, matrix products: 5.09 us -> none  [the longest x1 3.5 us: per_device(): jnp.einsum('arcs,csk->ark', gbar, column, precision=highest, preferred_el...]
    all_gather x1 -> x0, blocking collectives: 4.77 us -> none  [per_device(): stage = lax.all_gather(stage, 'core', axis=0, tiled=True)]
    another operation x10 -> x0, local copies, waits for them, and re-layouts: 4.6 us -> none
  transfers between devices with their start and end apart: 3 -> 3, of which waited for: 2 -> 3; matrix products, arithmetic and copies ran while one was open for 15% -> 0% of each run, Pallas kernels for 0% -> 6%
where the time goes in v2:
time: 125 us
  blocking collectives  60.8 us (49%)
  starting transfers between devices  24.8 us (20%)
  waiting for transfers between devices  22.2 us (18%)
  Pallas kernels  14.3 us (11%)
  local copies, waits for them, and re-layouts  2.02 us (2%)
    all_gather x1, blocking collectives, per_device(): along_z = lax.all_gather(own, 'z', axis=0)  31.9 us
    all_to_all x1, blocking collectives, per_device(): stage = lax.all_to_all(stage, near, 0, 0, tiled=True).reshape(width, width)  15.5 us
    pallas_call x6, Pallas kernels, call(): pl.pallas_call(kernel, out_shape=jax.tree.map(lambda s: jax.ShapeDtypeStr...  14.3 us
    all_to_all x1, blocking collectives, per_device(): slices = lax.all_to_all(corner, near, 0, 0, tiled=True)  13.4 us
    all_to_all x1, waiting for transfers between devices, per_device(): lax.all_to_all(call(fold_kernel, (n_z, count, width), slices), 'z', 0, 0,...  11.8 us
    all_to_all x1, starting transfers between devices, per_device(): lax.all_to_all(jnp.broadcast_to(along_z[None], (n_core,) + along_z.shape)...  11.8 us
    all_to_all x1, waiting for transfers between devices, per_device(): got = lax.all_to_all(sent, 'col', 0, 0, tiled=True)  8.67 us
    all_to_all x1, starting transfers between devices, per_device(): got = lax.all_to_all(sent, 'col', 0, 0, tiled=True)  6.89 us
  transfers between devices with their start and end apart: 3, of which 3 were waited for; matrix products, arithmetic and copies ran while one was open for 0% of the time, Pallas kernels for 6%

profile of v2, /device:TPU:1, one launch (start us, length us, event | category | flops | bytes accessed | tf_op | source)
XLA Modules:
  0.0 124.9 jit_solution(1039387555099804906)
XLA Ops:
  0.6 0.8 all_gather_reshape.3
  1.4 0.0 copy-start.2
  1.4 31.9 %all_gather.3 = f32[16,32,256]{2,1,0:T(8,128)S(1)} all-gather(f32[1,32,256]{2,1,0:T(8,128)S(1)} %all_gather_reshape.3), channel_id=1, replica_groups=mesh['z'=16,'core'=2,'col'=16] {'z'}, dimensions={0}, use_global_device_ids=true | all-gather | bytes 557056 | tf_op jit(solution)/shard_map/all_gather | solution.py:119
  33.3 1.1 broadcast_in_dim.17
  34.4 11.8 %all-to-all-start = ((f32[2,16,32,256]{3,2,1,0:T(8,128)}), f32[2,16,32,256]{3,2,1,0:T(8,128)S(1)}, u32[]{:S(2)}, u32[]{:S(2)}) async-start(f32[2,16,32,256]{3,2,1,0:T(8,128)} %broadcast_in_dim.17), calls=%async_computation | async-start | bytes 2097152 | tf_op jit(solution)/shard_map/all_to_all | solution.py:120
  46.2 1.7 %all-to-all-done.both_ref = f32[2,16,32,256]{3,2,1,0:T(8,128)S(1)} async-done(((f32[2,16,32,256]{3,2,1,0:T(8,128)}), f32[2,16,32,256]{3,2,1,0:T(8,128)S(1)}, u32[]{:S(2)}, u32[]{:S(2)}) %all-to-all-start) | async-done | bytes 1048608 | tf_op jit(solution)/shard_map/all_to_all | solution.py:120
  48.0 0.0 copy-done.2
  48.0 3.2 %shard_map.68 = f32[16,2,32,256]{3,2,1,0:T(8,128)} custom-call(s32[1]{0:T(128)} %bitcast.1.parity_ref, f32[4,1024,128]{2,1,0:T(8,128)S(1)} %bitcast.11, f32[2,16,32,256]{3,2,1,0:T(8,128)S(1)} %all-to-all-done.both_ref), custom_call_target="tpu_custom_call" | custom-call | flops 1600000000 | bytes 4194304 | tf_op jit(solution)/shard_map/pallas_call | solution.py:26
  51.2 0.0 copy-start
  51.2 6.9 %all-to-all-start.1 = ((f32[16,2,32,256]{3,2,1,0:T(8,128)}), f32[16,2,32,256]{3,2,1,0:T(8,128)S(1)}, u32[]{:S(2)}, u32[]{:S(2)}) async-start(f32[16,2,32,256]{3,2,1,0:T(8,128)} %shard_map.68), calls=%async_computation.1 | async-start | bytes 2097152 | tf_op jit(solution)/shard_map/all_to_all | solution.py:133
  58.1 0.0 copy-done
  58.1 0.0 copy-start.1
  58.1 7.6 %shard_map.69.inverse_ref = f32[256,256]{1,0:T(8,128)S(1)} custom-call(f32[256,256]{1,0:T(8,128)S(1)} %copy-done), custom_call_target="tpu_custom_call" | custom-call | flops 3200000000 | bytes 524288 | tf_op jit(solution)/shard_map/pallas_call | solution.py:26
  65.7 0.0 copy-start.3
  65.7 8.7 %all-to-all-done.1.got_ref = f32[16,2,32,256]{3,2,1,0:T(8,128)S(1)} async-done(((f32[16,2,32,256]{3,2,1,0:T(8,128)}), f32[16,2,32,256]{3,2,1,0:T(8,128)S(1)}, u32[]{:S(2)}, u32[]{:S(2)}) %all-to-all-start.1) | async-done | bytes 1048608 | tf_op jit(solution)/shard_map/all_to_all | solution.py:133
  74.4 0.0 copy-done.1
  74.4 1.0 shard_map.70
  75.3 13.4 %all_to_all.25.parts_ref = f32[32,8,256]{2,1,0:T(8,128)S(1)} all-to-all(f32[32,8,256]{2,1,0:T(8,128)S(1)} %get-tuple-element.5), channel_id=1, replica_groups=mesh['z'=16,'core'=2,'col'=16] {'core','col'}, dimensions={0} | all-to-all | bytes 524288 | tf_op jit(solution)/shard_map/all_to_all | solution.py:149
  88.8 0.7 shard_map.71
  89.5 6.1 %all-to-all-start.3 = ((f32[16,8,256]{2,1,0:T(8,128)}), f32[16,8,256]{2,1,0:T(8,128)S(1)}, u32[]{:S(2)}, u32[]{:S(2)}) async-start(f32[16,8,256]{2,1,0:T(8,128)} %shard_map.71), calls=%async_computation.3 | async-start | bytes 262144 | tf_op jit(solution)/shard_map/all_to_all | solution.py:150
  95.6 0.0 copy-done.3
  95.6 0.1 copy.8
  95.7 11.8 %all-to-all-done.3.parts_ref = f32[16,8,256]{2,1,0:T(8,128)S(1)} async-done(((f32[16,8,256]{2,1,0:T(8,128)}), f32[16,8,256]{2,1,0:T(8,128)S(1)}, u32[]{:S(2)}, u32[]{:S(2)}) %all-to-all-start.3) | async-done | bytes 131104 | tf_op jit(solution)/shard_map/all_to_all | solution.py:150
  107.5 0.6 shard_map.72
  108.2 15.5 %all_to_all.26 = f32[32,8,256]{2,1,0:T(8,128)S(1)} all-to-all(f32[32,8,256]{2,1,0:T(8,128)S(1)} %shard_map.72), channel_id=1, replica_groups=mesh['z'=16,'core'=2,'col'=16] {'core','col'}, dimensions={0} | all-to-all | bytes 524288 | tf_op jit(solution)/shard_map/all_to_all | solution.py:161
  123.7 1.2 shard_map.73
Async XLA Ops:
  1.4 46.6 %copy-start.2 = (f32[4,128,8,128]{3,2,1,0:T(8,128)S(1)}, f32[4,128,8,128]{3,2,1,0:T(8,128)}, u32[]{:S(2)}) copy-start(f32[4,128,8,128]{3,2,1,0:T(8,128)} %param.5) | copy-start | bytes 6291460
  34.4 13.5 %all-to-all-start = ((f32[2,16,32,256]{3,2,1,0:T(8,128)}), f32[2,16,32,256]{3,2,1,0:T(8,128)S(1)}, u32[]{:S(2)}, u32[]{:S(2)}) async-start(f32[2,16,32,256]{3,2,1,0:T(8,128)} %broadcast_in_dim.17), calls=%async_computation | async-start | bytes 2097152 | tf_op jit(solution)/shard_map/all_to_all | solution.py:120
  51.2 6.9 %copy-start = (f32[256,256]{1,0:T(8,128)S(1)}, f32[256,256]{1,0:T(8,128)}, u32[]{:S(2)}) copy-start(f32[256,256]{1,0:T(8,128)} %factor_ref.3) | copy-start | bytes 786436
  51.2 23.2 %all-to-all-start.1 = ((f32[16,2,32,256]{3,2,1,0:T(8,128)}), f32[16,2,32,256]{3,2,1,0:T(8,128)S(1)}, u32[]{:S(2)}, u32[]{:S(2)}) async-start(f32[16,2,32,256]{3,2,1,0:T(8,128)} %shard_map.68), calls=%async_computation.1 | async-start | bytes 2097152 | tf_op jit(solution)/shard_map/all_to_all | solution.py:133
  58.1 16.3 %copy-start.1 = (f32[4,8,256]{2,1,0:T(8,128)S(1)}, f32[4,8,256]{2,1,0:T(8,128)}, u32[]{:S(2)}) copy-start(f32[4,8,256]{2,1,0:T(8,128)} %param.7) | copy-start | bytes 98308
  65.7 29.9 %copy-start.3 = (f32[256,256]{1,0:T(8,128)S(1)}, f32[256,256]{1,0:T(8,128)}, u32[]{:S(2)}) copy-start(f32[256,256]{1,0:T(8,128)} %param.9) | copy-start | bytes 786436
  89.5 18.1 %all-to-all-start.3 = ((f32[16,8,256]{2,1,0:T(8,128)}), f32[16,8,256]{2,1,0:T(8,128)S(1)}, u32[]{:S(2)}, u32[]{:S(2)}) async-start(f32[16,8,256]{2,1,0:T(8,128)} %shard_map.71), calls=%async_computation.3 | async-start | bytes 262144 | tf_op jit(solution)/shard_map/all_to_all | solution.py:150

commit v3 on v2

--- a/solution.py
+++ b/solution.py
@@ -47,8 +47,8 @@
         size *= 2
 
 
-def product_kernel(parity_ref, gbar_ref, both_ref, out_ref, column_ref):
-    n_core, n_z, depth, width = both_ref.shape
+def product_kernel(where_ref, gbar_ref, both_ref, out_ref, column_ref):
+    n_core, _, _, depth, width = both_ref.shape
     col_blocks = column_ref.shape[0]
     row_blocks = gbar_ref.shape[0]
     part = depth // col_blocks
@@ -57,8 +57,10 @@
     share = out_ref.shape[2] // row_blocks
     n_col = out_ref.shape[0]
     for c in range(col_blocks):
-        for core in range(n_core):
-            column_ref[c, :, core * part:(core + 1) * part, :] = both_ref[core, :, c * part:(c + 1) * part, :]
+        for flip in range(2):
+            for core in range(n_core):
+                held = both_ref[where_ref[1] ^ (flip ^ core), :, flip, c * part:(c + 1) * part, :]
+                column_ref[c, :, flip, core * part:(core + 1) * part, :] = held
     full = column_ref[...].reshape(col_blocks * cols, width)
     for b in range(row_blocks):
         left = jnp.concatenate(
@@ -67,18 +69,22 @@
         out_ref[:, 0, b * share:(b + 1) * share, :] = dot(left, full).reshape(n_col, share, width)
     ratio = col_blocks // row_blocks
     for b in range(row_blocks):
-        local = column_ref[b * ratio + parity_ref[0]]
+        local = column_ref[b * ratio + where_ref[0]]
         out_ref[:, 1, b * share:(b + 1) * share, :] = local.reshape(n_col, share, width)
 
 
-def owned_kernel(source_ref, got_ref, adjoint_ref, inverse_ref, lower_ref, corner_ref):
+def owned_kernel(source_ref, got_ref, adjoint_ref, total_ref, corner_ref):
     n_col = got_ref.shape[0]
-    total = got_ref[0, 0]
+    product = got_ref[0, 0]
     for c in range(1, n_col):
-        total = total + got_ref[c, 0]
-    lower = dot(adjoint_ref[...] - 2.0 * total, inverse_ref[...])
-    lower_ref[...] = lower
-    corner_ref[...] = dot_tn(got_ref[source_ref[0], 1], lower).reshape(corner_ref.shape)
+        product = product + got_ref[c, 0]
+    total = adjoint_ref[...] - 2.0 * product
+    total_ref[...] = total
+    corner_ref[...] = dot_tn(got_ref[source_ref[0], 1], total).reshape(corner_ref.shape)
+
+
+def lower_kernel(total_ref, inverse_ref, out_ref):
+    out_ref[...] = dot(total_ref[...], inverse_ref[...])
 
 
 def fold_kernel(parts_ref, out_ref):
@@ -89,7 +95,8 @@
 def slice_kernel(begin_ref, parts_ref, adjoint_ref, factor_ref, inverse_ref, out_ref):
     count = out_ref.shape[1]
     begin = pl.multiple_of(begin_ref[0], count)
-    adjusted = adjoint_ref[pl.ds(begin, count), :] - jnp.sum(parts_ref[...], axis=0)
+    summed = dot(jnp.sum(parts_ref[...], axis=0), inverse_ref[...])
+    adjusted = adjoint_ref[pl.ds(begin, count), :] - summed
     projected = dot(adjusted, factor_ref[...])
     at_row = begin + lax.broadcasted_iota(jnp.int32, projected.shape, 0)
     at_col = lax.broadcasted_iota(jnp.int32, projected.shape, 1)
@@ -116,38 +123,45 @@
     n_near = n_core * n_col
     count = width // n_near
     own = panel.reshape(col_blocks * part, width)
-    along_z = lax.all_gather(own, "z", axis=0)
+    rings = [[2 * z + (z + start) % 2 for z in range(n_z)] for start in range(2)]
+    along_z = lax.all_gather(own, ("z", "core"), axis=0, axis_index_groups=rings)
     both = lax.all_to_all(
         jnp.broadcast_to(along_z[None], (n_core,) + along_z.shape), "core", 0, 0, tiled=True
     )
+    source = (row_at % n_col)[None]
+    adjoint = panel_adj.reshape(row_blocks * share, width)
+    both, source, adjoint = lax.optimization_barrier((both, source, adjoint))
     sent = call(
         product_kernel,
         (n_col, 2, row_blocks * share, width),
-        (row_at // n_col)[None],
+        jnp.stack([row_at // n_col, lax.axis_index("z") % 2]),
         gbar.reshape(row_blocks, rows * col_blocks, cols),
-        both,
-        scratch=[pltpu.VMEM((col_blocks, n_z, n_core * part, width), F32)],
+        both.reshape(n_core, n_z // 2, 2, col_blocks * part, width),
+        scratch=[pltpu.VMEM((col_blocks, n_z // 2, 2, n_core * part, width), F32)],
         scalars=1,
         cost=pl.CostEstimate(flops=int(1.6e9), bytes_accessed=4 << 20, transcendentals=0),
     )
     got = lax.all_to_all(sent, "col", 0, 0, tiled=True)
+    total, corner = call(
+        owned_kernel,
+        [(row_blocks * share, width), (n_near, count, width)],
+        source,
+        got,
+        adjoint,
+        scalars=1,
+    )
+    slices = lax.all_to_all(corner, near, 0, 0, tiled=True)
+    folded, factor = lax.optimization_barrier(
+        (call(fold_kernel, (n_z, count, width), slices), factor)
+    )
+    piece = lax.all_to_all(folded, "z", 0, 0, tiled=True)
     inverse = call(
         invert_kernel,
         (width, width),
         factor,
         cost=pl.CostEstimate(flops=int(3.2e9), bytes_accessed=1 << 19, transcendentals=0),
     )
-    lower, corner = call(
-        owned_kernel,
-        [(row_blocks * share, width), (n_near, count, width)],
-        (row_at % n_col)[None],
-        got,
-        panel_adj.reshape(row_blocks * share, width),
-        inverse,
-        scalars=1,
-    )
-    slices = lax.all_to_all(corner, near, 0, 0, tiled=True)
-    piece = lax.all_to_all(call(fold_kernel, (n_z, count, width), slices), "z", 0, 0, tiled=True)
+    lower = call(lower_kernel, (row_blocks * share, width), total, inverse)
     stage = call(
         slice_kernel,
         (n_near, count, width),

time: 125 us -> 122 us (0.976)
  blocking collectives: 60.8 us -> 72.5 us
  waiting for transfers between devices: 22.2 us -> 13.4 us
  starting transfers between devices: 24.8 us -> 17.5 us
    all_to_all x2, waiting for transfers between devices: 20.5 us -> 11.7 us  [the longest x1 7.45 us: per_device(): stage = lax.all_to_all(stage, near, 0, 0, tiled=True).reshape(width, width)]
    all_to_all x1, starting transfers between devices: 11.8 us -> 3.69 us  [per_device(): lax.all_to_all(jnp.broadcast_to(along_z[None], (n_core,) + along_z.shape)...]
    all_to_all x1, blocking collectives: 15.5 us -> 23 us  [per_device(): got = lax.all_to_all(sent, 'col', 0, 0, tiled=True)]
    all_gather x1, blocking collectives: 31.9 us -> 36.4 us  [per_device(): lax.all_gather(own, ('z', 'core'), axis=0, axis_index_groups=rings)]
    pallas_call x6 -> x7, Pallas kernels: 14.3 us -> 15.1 us  [call(): pl.pallas_call(kernel, out_shape=jax.tree.map(lambda s: jax.ShapeDtypeStr...]
  transfers between devices with their start and end apart: 3 -> 3, of which waited for: 3 -> 3; matrix products, arithmetic and copies ran while one was open for 0% -> 0% of each run, Pallas kernels for 6% -> 7%
where the time goes in v3:
time: 122 us; the launch traced here: 121 us
  blocking collectives  72.5 us (59%)
  starting transfers between devices  17.5 us (14%)
  Pallas kernels  15.1 us (12%)
  waiting for transfers between devices  13.4 us (11%)
  local copies, waits for them, and re-layouts  2.03 us (2%)
    all_gather x1, blocking collectives, per_device(): lax.all_gather(own, ('z', 'core'), axis=0, axis_index_groups=rings)  36.4 us
    all_to_all x1, blocking collectives, per_device(): got = lax.all_to_all(sent, 'col', 0, 0, tiled=True)  23 us
    pallas_call x7, Pallas kernels, call(): pl.pallas_call(kernel, out_shape=jax.tree.map(lambda s: jax.ShapeDtypeStr...  15.1 us
    all_to_all x1, blocking collectives, per_device(): slices = lax.all_to_all(corner, near, 0, 0, tiled=True)  13.1 us
    all_to_all x1, waiting for transfers between devices, per_device(): stage = lax.all_to_all(stage, near, 0, 0, tiled=True).reshape(width, width)  7.45 us
    all_to_all x1, starting transfers between devices, per_device(): stage = lax.all_to_all(stage, near, 0, 0, tiled=True).reshape(width, width)  7.39 us
    all_to_all x1, starting transfers between devices, per_device(): piece = lax.all_to_all(folded, 'z', 0, 0, tiled=True)  6.44 us
    all_to_all x1, waiting for transfers between devices, per_device(): piece = lax.all_to_all(folded, 'z', 0, 0, tiled=True)  4.2 us
  transfers between devices with their start and end apart: 3, of which 3 were waited for; matrix products, arithmetic and copies ran while one was open for 0% of the time, Pallas kernels for 7%

profile of v3, /device:TPU:1, one launch (start us, length us, event | category | flops | bytes accessed | tf_op | source)
XLA Modules:
  0.0 121.4 jit_solution(130422245720176848)
XLA Ops:
  0.6 0.8 all_gather_reshape.3
  1.4 0.0 copy-start.2
  1.4 36.4 %all_gather.3 = f32[16,32,256]{2,1,0:T(8,128)S(1)} all-gather(f32[1,32,256]{2,1,0:T(8,128)S(1)} %all_gather_reshape.3), channel_id=1, replica_groups={{0,48,64,112,128,176,192,240,256,304,320,368,384,432,448,496},{16,32,80..., dimensions={0}, use_global_device_ids=true | all-gather | bytes 557056 | tf_op jit(solution)/shard_map/all_gather | solution.py:127
  37.9 1.1 broadcast_in_dim.12
  39.0 3.7 %all-to-all-start = ((f32[2,16,32,256]{3,2,1,0:T(8,128)}), f32[2,16,32,256]{3,2,1,0:T(8,128)S(1)}, u32[]{:S(2)}, u32[]{:S(2)}) async-start(f32[2,16,32,256]{3,2,1,0:T(8,128)} %broadcast_in_dim.12), calls=%async_computation | async-start | bytes 2097152 | tf_op jit(solution)/shard_map/all_to_all | solution.py:128
  42.7 1.7 %all-to-all-done = f32[2,16,32,256]{3,2,1,0:T(8,128)S(1)} async-done(((f32[2,16,32,256]{3,2,1,0:T(8,128)}), f32[2,16,32,256]{3,2,1,0:T(8,128)S(1)}, u32[]{:S(2)}, u32[]{:S(2)}) %all-to-all-start) | async-done | bytes 1048608 | tf_op jit(solution)/shard_map/all_to_all | solution.py:128
  44.4 0.1 pad_add_fusion.where_ref
  44.5 0.0 copy-done.2
  44.5 2.8 %shard_map.68 = f32[16,2,32,256]{3,2,1,0:T(8,128)S(1)} custom-call(s32[2]{0:T(128)S(1)} %pad_add_fusion.where_ref, f32[4,1024,128]{2,1,0:T(8,128)S(1)} %bitcast.14, f32[2,8,2,32,256]{4,3,2,1,0:T(8,128)S(1)} %bitcast.11), custom_call_target="tpu_custom_call" | custom-call | flops 1600000000 | bytes 4194304 | tf_op jit(solution)/shard_map/pallas_call | solution.py:26
  47.2 0.0 copy-start.1
  47.3 0.0 copy-start.3
  47.3 0.0 copy-start
  47.3 23.0 %all_to_all.25.got_ref = f32[16,2,32,256]{3,2,1,0:T(8,128)S(1)} all-to-all(f32[16,2,32,256]{3,2,1,0:T(8,128)S(1)} %shard_map.68), channel_id=1, replica_groups=mesh['z'=16,'core'=2,'col'=16] {'col'}, dimensions={0} | all-to-all | bytes 2097152 | tf_op jit(solution)/shard_map/all_to_all | solution.py:144
  70.3 0.0 copy-done.1
  70.3 0.4 shard_map.69
  70.7 13.1 %all_to_all.26.parts_ref = f32[32,8,256]{2,1,0:T(8,128)S(1)} all-to-all(f32[32,8,256]{2,1,0:T(8,128)S(1)} %get-tuple-element.13), channel_id=1, replica_groups=mesh['z'=16,'core'=2,'col'=16] {'core','col'}, dimensions={0} | all-to-all | bytes 524288 | tf_op jit(solution)/shard_map/all_to_all | solution.py:153
  83.8 0.7 shard_map.70
  84.5 6.4 %all-to-all-start.3 = ((f32[16,8,256]{2,1,0:T(8,128)}), f32[16,8,256]{2,1,0:T(8,128)S(1)}, u32[]{:S(2)}, u32[]{:S(2)}) async-start(f32[16,8,256]{2,1,0:T(8,128)} %shard_map.70), calls=%async_computation.3 | async-start | bytes 262144 | tf_op jit(solution)/shard_map/all_to_all | solution.py:157
  90.9 0.0 copy-done.3
  91.0 0.1 copy.8
  91.1 0.0 copy-done
  91.1 7.6 %shard_map.71.inverse_ref = f32[256,256]{1,0:T(8,128)S(1)} custom-call(f32[256,256]{1,0:T(8,128)S(1)} %copy-done), custom_call_target="tpu_custom_call" | custom-call | flops 3200000000 | bytes 524288 | tf_op jit(solution)/shard_map/pallas_call | solution.py:26
  98.7 4.2 %all-to-all-done.3.parts_ref = f32[16,8,256]{2,1,0:T(8,128)S(1)} async-done(((f32[16,8,256]{2,1,0:T(8,128)}), f32[16,8,256]{2,1,0:T(8,128)S(1)}, u32[]{:S(2)}, u32[]{:S(2)}) %all-to-all-start.3) | async-done | bytes 131104 | tf_op jit(solution)/shard_map/all_to_all | solution.py:157
  102.9 1.5 %shard_map.73 = f32[32,8,256]{2,1,0:T(8,128)} custom-call(s32[1]{0:T(128)} %bitcast.7.begin_ref, f32[16,8,256]{2,1,0:T(8,128)S(1)} %all-to-all-done.3.parts_ref, f32[256,256]{1,0:T(8,128)S(1)} %bitcast.12, f32[256,256]{1,0:T(8,128)S(1)} %copy-done, f32[256,256]{1,0:T(8,128)S(1)} %shard_map.71.inverse_ref), custom_call_target="tpu_custom_call" | custom-call | tf_op jit(solution)/shard_map/pallas_call | solution.py:26
  104.5 7.4 %all-to-all-start.4 = ((f32[32,8,256]{2,1,0:T(8,128)}), f32[32,8,256]{2,1,0:T(8,128)S(1)}, u32[]{:S(2)}, u32[]{:S(2)}) async-start(f32[32,8,256]{2,1,0:T(8,128)} %shard_map.73), calls=%async_computation.4 | async-start | bytes 524288 | tf_op jit(solution)/shard_map/all_to_all | solution.py:175
  111.9 0.8 shard_map.72
  112.7 7.4 %all-to-all-done.4 = f32[32,8,256]{2,1,0:T(8,128)S(1)} async-done(((f32[32,8,256]{2,1,0:T(8,128)}), f32[32,8,256]{2,1,0:T(8,128)S(1)}, u32[]{:S(2)}, u32[]{:S(2)}) %all-to-all-start.4) | async-done | bytes 262176 | tf_op jit(solution)/shard_map/all_to_all | solution.py:175
  120.2 1.2 shard_map.74
Async XLA Ops:
  1.4 43.1 %copy-start.2 = (f32[4,128,8,128]{3,2,1,0:T(8,128)S(1)}, f32[4,128,8,128]{3,2,1,0:T(8,128)}, u32[]{:S(2)}) copy-start(f32[4,128,8,128]{3,2,1,0:T(8,128)} %param.5) | copy-start | bytes 6291460
  39.0 5.4 %all-to-all-start = ((f32[2,16,32,256]{3,2,1,0:T(8,128)}), f32[2,16,32,256]{3,2,1,0:T(8,128)S(1)}, u32[]{:S(2)}, u32[]{:S(2)}) async-start(f32[2,16,32,256]{3,2,1,0:T(8,128)} %broadcast_in_dim.12), calls=%async_computation | async-start | bytes 2097152 | tf_op jit(solution)/shard_map/all_to_all | solution.py:128
  47.2 23.1 %copy-start.1 = (f32[4,8,256]{2,1,0:T(8,128)S(1)}, f32[4,8,256]{2,1,0:T(8,128)}, u32[]{:S(2)}) copy-start(f32[4,8,256]{2,1,0:T(8,128)} %param.7) | copy-start | bytes 98308
  47.3 43.7 %copy-start.3 = (f32[256,256]{1,0:T(8,128)S(1)}, f32[256,256]{1,0:T(8,128)}, u32[]{:S(2)}) copy-start(f32[256,256]{1,0:T(8,128)} %param.9) | copy-start | bytes 786436
  47.3 43.8 %copy-start = (f32[256,256]{1,0:T(8,128)S(1)}, f32[256,256]{1,0:T(8,128)}, u32[]{:S(2)}) copy-start(f32[256,256]{1,0:T(8,128)} %factor_ref.1) | copy-start | bytes 786436
  84.5 18.4 %all-to-all-start.3 = ((f32[16,8,256]{2,1,0:T(8,128)}), f32[16,8,256]{2,1,0:T(8,128)S(1)}, u32[]{:S(2)}, u32[]{:S(2)}) async-start(f32[16,8,256]{2,1,0:T(8,128)} %shard_map.70), calls=%async_computation.3 | async-start | bytes 262144 | tf_op jit(solution)/shard_map/all_to_all | solution.py:157
  104.5 15.7 %all-to-all-start.4 = ((f32[32,8,256]{2,1,0:T(8,128)}), f32[32,8,256]{2,1,0:T(8,128)S(1)}, u32[]{:S(2)}, u32[]{:S(2)}) async-start(f32[32,8,256]{2,1,0:T(8,128)} %shard_map.73), calls=%async_computation.4 | async-start | bytes 524288 | tf_op jit(solution)/shard_map/all_to_all | solution.py:175

commit v4 on v3

--- a/solution.py
+++ b/solution.py
@@ -47,11 +47,10 @@
         size *= 2
 
 
-def product_kernel(where_ref, gbar_ref, both_ref, out_ref, column_ref):
-    n_core, _, _, depth, width = both_ref.shape
+def product_kernel(parity_ref, turn_ref, gbar_ref, first_ref, second_ref, out_ref, column_ref):
+    n_core, pairs, _, _, part, width = first_ref.shape
     col_blocks = column_ref.shape[0]
     row_blocks = gbar_ref.shape[0]
-    part = depth // col_blocks
     cols = gbar_ref.shape[2]
     rows = gbar_ref.shape[1] // col_blocks
     share = out_ref.shape[2] // row_blocks
@@ -59,8 +58,9 @@
     for c in range(col_blocks):
         for flip in range(2):
             for core in range(n_core):
-                held = both_ref[where_ref[1] ^ (flip ^ core), :, flip, c * part:(c + 1) * part, :]
-                column_ref[c, :, flip, core * part:(core + 1) * part, :] = held
+                for at, from_ref in ((0, first_ref), (pairs, second_ref)):
+                    held = from_ref[turn_ref[0] ^ (flip ^ core), :, flip, c]
+                    column_ref[c, at:at + pairs, flip, core * part:(core + 1) * part, :] = held
     full = column_ref[...].reshape(col_blocks * cols, width)
     for b in range(row_blocks):
         left = jnp.concatenate(
@@ -69,7 +69,7 @@
         out_ref[:, 0, b * share:(b + 1) * share, :] = dot(left, full).reshape(n_col, share, width)
     ratio = col_blocks // row_blocks
     for b in range(row_blocks):
-        local = column_ref[b * ratio + where_ref[0]]
+        local = column_ref[b * ratio + parity_ref[0]]
         out_ref[:, 1, b * share:(b + 1) * share, :] = local.reshape(n_col, share, width)
 
 
@@ -83,8 +83,9 @@
     corner_ref[...] = dot_tn(got_ref[source_ref[0], 1], total).reshape(corner_ref.shape)
 
 
-def lower_kernel(total_ref, inverse_ref, out_ref):
+def lower_kernel(total_ref, inverse_ref, adjoint_ref, factor_ref, out_ref, known_ref):
     out_ref[...] = dot(total_ref[...], inverse_ref[...])
+    known_ref[...] = dot_tn(adjoint_ref[...], factor_ref[...])
 
 
 def fold_kernel(parts_ref, out_ref):
@@ -92,12 +93,10 @@
     out_ref[...] = jnp.broadcast_to(total[None], out_ref.shape)
 
 
-def slice_kernel(begin_ref, parts_ref, adjoint_ref, factor_ref, inverse_ref, out_ref):
+def slice_kernel(begin_ref, parts_ref, known_ref, inverse_ref, out_ref):
     count = out_ref.shape[1]
     begin = pl.multiple_of(begin_ref[0], count)
-    summed = dot(jnp.sum(parts_ref[...], axis=0), inverse_ref[...])
-    adjusted = adjoint_ref[pl.ds(begin, count), :] - summed
-    projected = dot(adjusted, factor_ref[...])
+    projected = known_ref[pl.ds(begin, count), :] - jnp.sum(parts_ref[...], axis=0)
     at_row = begin + lax.broadcasted_iota(jnp.int32, projected.shape, 0)
     at_col = lax.broadcasted_iota(jnp.int32, projected.shape, 1)
     halved = jnp.where(at_row < at_col, projected, jnp.where(at_row == at_col, 0.5 * projected, 0.0))
@@ -122,23 +121,24 @@
     near = ("core", "col")
     n_near = n_core * n_col
     count = width // n_near
-    own = panel.reshape(col_blocks * part, width)
     rings = [[2 * z + (z + start) % 2 for z in range(n_z)] for start in range(2)]
-    along_z = lax.all_gather(own, ("z", "core"), axis=0, axis_index_groups=rings)
-    both = lax.all_to_all(
-        jnp.broadcast_to(along_z[None], (n_core,) + along_z.shape), "core", 0, 0, tiled=True
-    )
+    along_z = lax.all_gather(panel, ("z", "core"), axis=0, axis_index_groups=rings, tiled=True)
+    middle = n_z * col_blocks // 2
+    first = lax.all_gather(along_z[:middle], "core", axis=0, tiled=True)
+    rest, first = lax.optimization_barrier((along_z[middle:], first))
+    both = [first, lax.all_gather(rest, "core", axis=0, tiled=True)]
     source = (row_at % n_col)[None]
     adjoint = panel_adj.reshape(row_blocks * share, width)
-    both, source, adjoint = lax.optimization_barrier((both, source, adjoint))
+    *both, source, adjoint = lax.optimization_barrier((*both, source, adjoint))
     sent = call(
         product_kernel,
         (n_col, 2, row_blocks * share, width),
-        jnp.stack([row_at // n_col, lax.axis_index("z") % 2]),
+        (row_at // n_col)[None],
+        (lax.axis_index("z") % 2)[None],
         gbar.reshape(row_blocks, rows * col_blocks, cols),
-        both.reshape(n_core, n_z // 2, 2, col_blocks * part, width),
+        *[b.reshape(n_core, n_z // 4, 2, col_blocks, part, width) for b in both],
         scratch=[pltpu.VMEM((col_blocks, n_z // 2, 2, n_core * part, width), F32)],
-        scalars=1,
+        scalars=2,
         cost=pl.CostEstimate(flops=int(1.6e9), bytes_accessed=4 << 20, transcendentals=0),
     )
     got = lax.all_to_all(sent, "col", 0, 0, tiled=True)
@@ -161,14 +161,20 @@
         factor,
         cost=pl.CostEstimate(flops=int(3.2e9), bytes_accessed=1 << 19, transcendentals=0),
     )
-    lower = call(lower_kernel, (row_blocks * share, width), total, inverse)
+    lower, known = call(
+        lower_kernel,
+        [(row_blocks * share, width), (width, width)],
+        total,
+        inverse,
+        factor_adj,
+        factor,
+    )
     stage = call(
         slice_kernel,
         (n_near, count, width),
         ((core_at * n_col + col_at) * count)[None],
         piece,
-        factor_adj.T,
-        factor,
+        known,
         inverse,
         scalars=1,
     )

time: 122 us -> 117 us (0.959)
  blocking collectives: 72.5 us -> 92.5 us
  starting transfers between devices: 17.5 us -> 6.45 us
  waiting for transfers between devices: 13.4 us -> 3.33 us
  local copies, waits for them, and re-layouts: 2.03 us -> 0.06 us
  Pallas kernels: 15.1 us -> 13.3 us
    all_to_all x0 -> x1, blocking collectives: none -> 15.5 us  [per_device(): stage = lax.all_to_all(stage, near, 0, 0, tiled=True).reshape(width, width)]
    all_to_all x2 -> x0, starting transfers between devices: 11.1 us -> none  [the longest x1 7.39 us: per_device(): stage = lax.all_to_all(stage, near, 0, 0, tiled=True).reshape(width, width)]
    all_to_all x2 -> x0, waiting for transfers between devices: 9.19 us -> none  [the longest x1 7.45 us: per_device(): stage = lax.all_to_all(stage, near, 0, 0, tiled=True).reshape(width, width)]
    all_gather x1 -> x3, blocking collectives: 36.4 us -> 41 us  [the longest x1 36.7 us: per_device(): lax.all_gather(panel, ('z', 'core'), axis=0, axis_index_groups=rings, til...]
    pallas_call x7, Pallas kernels: 15.1 us -> 13.3 us  [call(): pl.pallas_call(kernel, out_shape=jax.tree.map(lambda s: jax.ShapeDtypeStr...]
  transfers between devices with their start and end apart: 3 -> 1, of which waited for: 3 -> 1; matrix products, arithmetic and copies ran while one was open for 0% -> 0% of each run, Pallas kernels for 7% -> 7%
where the time goes in v4:
time: 117 us; the launch traced here: 116 us
  blocking collectives  92.5 us (79%)
  Pallas kernels  13.3 us (11%)
  starting transfers between devices  6.45 us (6%)
  waiting for transfers between devices  3.33 us (3%)
    all_gather x1, blocking collectives, per_device(): lax.all_gather(panel, ('z', 'core'), axis=0, axis_index_groups=rings, til...  36.7 us
    all_to_all x1, blocking collectives, per_device(): got = lax.all_to_all(sent, 'col', 0, 0, tiled=True)  23.3 us
    all_to_all x1, blocking collectives, per_device(): stage = lax.all_to_all(stage, near, 0, 0, tiled=True).reshape(width, width)  15.5 us
    pallas_call x7, Pallas kernels, call(): pl.pallas_call(kernel, out_shape=jax.tree.map(lambda s: jax.ShapeDtypeStr...  13.3 us
    all_to_all x1, blocking collectives, per_device(): slices = lax.all_to_all(corner, near, 0, 0, tiled=True)  12.7 us
    all_to_all x1, starting transfers between devices, per_device(): piece = lax.all_to_all(folded, 'z', 0, 0, tiled=True)  6.45 us
    all_to_all x1, waiting for transfers between devices, per_device(): piece = lax.all_to_all(folded, 'z', 0, 0, tiled=True)  3.33 us
  transfers between devices with their start and end apart: 1, of which 1 were waited for; matrix products, arithmetic and copies ran while one was open for 0% of the time, Pallas kernels for 7%

profile of v4, /device:TPU:1, one launch (start us, length us, event | category | flops | bytes accessed | tf_op | source)
XLA Modules:
  0.0 116.4 jit_solution(4454734664774932524)
XLA Ops:
  0.6 0.0 copy-start.3
  0.7 36.7 %all_gather.9 = f32[128,4,256]{2,1,0:T(4,128)S(1)} all-gather(f32[8,4,256]{2,1,0:T(4,128)} %param.6), channel_id=1, replica_groups={{0,48,64,112,128,176,192,240,256,304,320,368,384,432,448,496},{16,32,80..., dimensions={0}, use_global_device_ids=true | all-gather | bytes 557056 | tf_op jit(solution)/shard_map/all_gather | solution.py:125
  37.4 2.2 %all_gather.10 = f32[128,4,256]{2,1,0:T(4,128)S(1)} all-gather(f32[64,4,256]{2,1,0:T(4,128)S(1)} %get-tuple-element.26), channel_id=1, replica_groups=mesh['z'=16,'core'=2,'col'=16] {'core'}, dimensions={0}, use_global_device_ids=true | all-gather | bytes 786432 | tf_op jit(solution)/shard_map/all_gather | solution.py:127
  39.6 2.2 %all_gather.11 = f32[128,4,256]{2,1,0:T(4,128)S(1)} all-gather(f32[64,4,256]{2,1,0:T(4,128)S(1)} %get-tuple-element.15), channel_id=1, replica_groups=mesh['z'=16,'core'=2,'col'=16] {'core'}, dimensions={0}, use_global_device_ids=true | all-gather | bytes 786432 | tf_op jit(solution)/shard_map/all_gather | solution.py:129
  41.7 0.0 copy-done.3
  41.7 2.2 %shard_map.68 = f32[16,2,32,256]{3,2,1,0:T(8,128)S(1)} custom-call(s32[1]{0:T(128)} %bitcast.2.parity_ref, s32[1]{0:T(128)} %bitcast.3.turn_ref, f32[4,1024,128]{2,1,0:T(8,128)S(1)} %bitcast.14, f32[2,4,2,8,4,256]{5,4,3,2,1,0:T(4,128)S(1)} %bitcast.11, f32[2,4,2,8,4,256]{5,4,3,2,1,0:T(4,128)S(1)} %bitcast.12), custom_call_target="tpu_custom_call" | custom-call | flops 1600000000 | bytes 4194304 | tf_op jit(solution)/shard_map/pallas_call | solution.py:26
  43.9 0.0 copy-start.2
  43.9 0.0 copy-start
  43.9 23.3 %all_to_all.20.got_ref = f32[16,2,32,256]{3,2,1,0:T(8,128)S(1)} all-to-all(f32[16,2,32,256]{3,2,1,0:T(8,128)S(1)} %shard_map.68), channel_id=1, replica_groups=mesh['z'=16,'core'=2,'col'=16] {'col'}, dimensions={0} | all-to-all | bytes 2097152 | tf_op jit(solution)/shard_map/all_to_all | solution.py:144
  67.2 0.0 copy-done.2
  67.2 0.4 shard_map.69
  67.6 12.7 %all_to_all.21.parts_ref = f32[32,8,256]{2,1,0:T(8,128)S(1)} all-to-all(f32[32,8,256]{2,1,0:T(8,128)S(1)} %get-tuple-element.21), channel_id=1, replica_groups=mesh['z'=16,'core'=2,'col'=16] {'core','col'}, dimensions={0} | all-to-all | bytes 524288 | tf_op jit(solution)/shard_map/all_to_all | solution.py:153
  80.3 0.7 shard_map.70
  81.0 6.4 %all-to-all-start.2 = ((f32[16,8,256]{2,1,0:T(8,128)}), f32[16,8,256]{2,1,0:T(8,128)S(1)}, u32[]{:S(2)}, u32[]{:S(2)}) async-start(f32[16,8,256]{2,1,0:T(8,128)} %shard_map.70), calls=%async_computation.2 | async-start | bytes 262144 | tf_op jit(solution)/shard_map/all_to_all | solution.py:157
  87.5 0.0 copy-done
  87.5 0.0 copy-start.1
  87.5 7.6 %shard_map.71.inverse_ref = f32[256,256]{1,0:T(8,128)S(1)} custom-call(f32[256,256]{1,0:T(8,128)S(1)} %copy-done), custom_call_target="tpu_custom_call" | custom-call | flops 3200000000 | bytes 524288 | tf_op jit(solution)/shard_map/pallas_call | solution.py:26
  95.1 0.0 copy-done.1
  95.1 1.0 shard_map.72
  96.1 3.3 %all-to-all-done.2.parts_ref = f32[16,8,256]{2,1,0:T(8,128)S(1)} async-done(((f32[16,8,256]{2,1,0:T(8,128)}), f32[16,8,256]{2,1,0:T(8,128)S(1)}, u32[]{:S(2)}, u32[]{:S(2)}) %all-to-all-start.2) | async-done | bytes 131104 | tf_op jit(solution)/shard_map/all_to_all | solution.py:157
  99.5 0.2 shard_map.73
  99.7 15.5 %all_to_all.22 = f32[32,8,256]{2,1,0:T(8,128)S(1)} all-to-all(f32[32,8,256]{2,1,0:T(8,128)S(1)} %shard_map.73), channel_id=1, replica_groups=mesh['z'=16,'core'=2,'col'=16] {'core','col'}, dimensions={0} | all-to-all | bytes 524288 | tf_op jit(solution)/shard_map/all_to_all | solution.py:181
  115.2 1.2 %shard_map.74 = f32[256,256]{1,0:T(8,128)} custom-call(f32[256,256]{1,0:T(8,128)S(1)} %bitcast.10, f32[256,256]{1,0:T(8,128)S(1)} %shard_map.71.inverse_ref), custom_call_target="tpu_custom_call" | custom-call | tf_op jit(solution)/shard_map/pallas_call | solution.py:26
  (1 shorter events, 0.0 us)
Async XLA Ops:
  0.6 41.1 %copy-start.3 = (f32[4,128,8,128]{3,2,1,0:T(8,128)S(1)}, f32[4,128,8,128]{3,2,1,0:T(8,128)}, u32[]{:S(2)}) copy-start(f32[4,128,8,128]{3,2,1,0:T(8,128)} %param.5) | copy-start | bytes 6291460
  43.9 23.3 %copy-start.2 = (f32[4,8,256]{2,1,0:T(8,128)S(1)}, f32[4,8,256]{2,1,0:T(8,128)}, u32[]{:S(2)}) copy-start(f32[4,8,256]{2,1,0:T(8,128)} %param.7) | copy-start | bytes 98308
  43.9 43.6 %copy-start = (f32[256,256]{1,0:T(8,128)S(1)}, f32[256,256]{1,0:T(8,128)}, u32[]{:S(2)}) copy-start(f32[256,256]{1,0:T(8,128)} %factor_ref.1) | copy-start | bytes 786436
  81.0 18.4 %all-to-all-start.2 = ((f32[16,8,256]{2,1,0:T(8,128)}), f32[16,8,256]{2,1,0:T(8,128)S(1)}, u32[]{:S(2)}, u32[]{:S(2)}) async-start(f32[16,8,256]{2,1,0:T(8,128)} %shard_map.70), calls=%async_computation.2 | async-start | bytes 262144 | tf_op jit(solution)/shard_map/all_to_all | solution.py:157
  87.5 7.6 %copy-start.1 = (f32[256,256]{1,0:T(8,128)S(1)}, f32[256,256]{1,0:T(8,128)}, u32[]{:S(2)}) copy-start(f32[256,256]{1,0:T(8,128)} %adjoint_ref.1) | copy-start | bytes 786436

commit v5 on v4

--- a/solution.py
+++ b/solution.py
@@ -1,3 +1,5 @@
+import functools
+
 import jax
 import jax.numpy as jnp
 from jax import lax
@@ -47,13 +49,13 @@
         size *= 2
 
 
-def product_kernel(parity_ref, turn_ref, gbar_ref, first_ref, second_ref, out_ref, column_ref):
+def product_kernel(parity_ref, turn_ref, core_ref, gbar_ref, first_ref, second_ref, out_ref, column_ref):
     n_core, pairs, _, _, part, width = first_ref.shape
     col_blocks = column_ref.shape[0]
     row_blocks = gbar_ref.shape[0]
     cols = gbar_ref.shape[2]
     rows = gbar_ref.shape[1] // col_blocks
-    share = out_ref.shape[2] // row_blocks
+    share = rows // out_ref.shape[0]
     n_col = out_ref.shape[0]
     for c in range(col_blocks):
         for flip in range(2):
@@ -66,21 +68,29 @@
         left = jnp.concatenate(
             [gbar_ref[b, pl.ds(c, rows, stride=col_blocks), :] for c in range(col_blocks)], axis=1
         )
-        out_ref[:, 0, b * share:(b + 1) * share, :] = dot(left, full).reshape(n_col, share, width)
+        out_ref[:, b * share:(b + 1) * share, :] = dot(left, full).reshape(n_col, share, width)
     ratio = col_blocks // row_blocks
     for b in range(row_blocks):
-        local = column_ref[b * ratio + parity_ref[0]]
-        out_ref[:, 1, b * share:(b + 1) * share, :] = local.reshape(n_col, share, width)
-
-
-def owned_kernel(source_ref, got_ref, adjoint_ref, total_ref, corner_ref):
-    n_col = got_ref.shape[0]
-    product = got_ref[0, 0]
-    for c in range(1, n_col):
-        product = product + got_ref[c, 0]
-    total = adjoint_ref[...] - 2.0 * product
-    total_ref[...] = total
-    corner_ref[...] = dot_tn(got_ref[source_ref[0], 1], total).reshape(corner_ref.shape)
+        local = column_ref[b * ratio + parity_ref[0]].reshape(n_col, share, width)
+        at = row_blocks * share + b * part
+        out_ref[:, at:at + part, :] = jnp.where(core_ref[0] == 0, local[:, :part], local[:, part:])
+
+
+def owned_kernel(source_ref, got_ref, adjoint_ref, total_ref, halves_ref):
+    owned = adjoint_ref.shape[0]
+    total_ref[...] = adjoint_ref[...] - 2.0 * jnp.sum(got_ref[:, :owned, :], axis=0)
+    for core in range(halves_ref.shape[0]):
+        halves_ref[core] = got_ref[source_ref[0] + core, owned:, :]
+
+
+def corner_kernel(part, core_ref, halves_ref, total_ref, corner_ref, mine_ref):
+    n_core, _, half, _ = halves_ref.shape
+    for core in range(n_core):
+        rows = halves_ref[core, core_ref[0]]
+        for b in range(half // part):
+            at = (b * n_core + core) * part
+            mine_ref[at:at + part, :] = rows[b * part:(b + 1) * part]
+    corner_ref[...] = dot_tn(mine_ref[...], total_ref[...]).reshape(corner_ref.shape)
 
 
 def lower_kernel(total_ref, inverse_ref, adjoint_ref, factor_ref, out_ref, known_ref):
@@ -127,27 +137,38 @@
     first = lax.all_gather(along_z[:middle], "core", axis=0, tiled=True)
     rest, first = lax.optimization_barrier((along_z[middle:], first))
     both = [first, lax.all_gather(rest, "core", axis=0, tiled=True)]
-    source = (row_at % n_col)[None]
+    source = (lax.axis_index("z") * n_core % n_col)[None]
+    core = core_at[None]
     adjoint = panel_adj.reshape(row_blocks * share, width)
-    *both, source, adjoint = lax.optimization_barrier((*both, source, adjoint))
+    *both, source, core, adjoint = lax.optimization_barrier((*both, source, core, adjoint))
     sent = call(
         product_kernel,
-        (n_col, 2, row_blocks * share, width),
+        (n_col, row_blocks * (share + part), width),
         (row_at // n_col)[None],
         (lax.axis_index("z") % 2)[None],
+        core,
         gbar.reshape(row_blocks, rows * col_blocks, cols),
         *[b.reshape(n_core, n_z // 4, 2, col_blocks, part, width) for b in both],
         scratch=[pltpu.VMEM((col_blocks, n_z // 2, 2, n_core * part, width), F32)],
-        scalars=2,
+        scalars=3,
         cost=pl.CostEstimate(flops=int(1.6e9), bytes_accessed=4 << 20, transcendentals=0),
     )
     got = lax.all_to_all(sent, "col", 0, 0, tiled=True)
-    total, corner = call(
+    total, halves = call(
         owned_kernel,
-        [(row_blocks * share, width), (n_near, count, width)],
+        [(row_blocks * share, width), (n_core, row_blocks * part, width)],
         source,
         got,
         adjoint,
+        scalars=1,
+    )
+    corner = call(
+        functools.partial(corner_kernel, part),
+        (n_near, count, width),
+        core,
+        lax.all_gather(halves, "core", axis=0),
+        total,
+        scratch=[pltpu.VMEM((row_blocks * share, width), F32)],
         scalars=1,
     )
     slices = lax.all_to_all(corner, near, 0, 0, tiled=True)

time: 117 us -> 116 us (level)
    all_gather x0 -> x1, blocking collectives: none -> 2.77 us  [per_device(): lax.all_gather(halves, 'core', axis=0)]
    all_to_all x1, blocking collectives: 23.3 us -> 20.7 us  [per_device(): got = lax.all_to_all(sent, 'col', 0, 0, tiled=True)]
    pallas_call x7 -> x8, Pallas kernels: 13.3 us -> 13.4 us  [call(): pl.pallas_call(kernel, out_shape=jax.tree.map(lambda s: jax.ShapeDtypeStr...]
where the time goes in v5:
time: 116 us
  blocking collectives  91.6 us (79%)
  Pallas kernels  13.4 us (12%)
  starting transfers between devices  6.43 us (6%)
  waiting for transfers between devices  3.33 us (3%)
    all_gather x1, blocking collectives, per_device(): lax.all_gather(panel, ('z', 'core'), axis=0, axis_index_groups=rings, til...  36.7 us
    all_to_all x1, blocking collectives, per_device(): got = lax.all_to_all(sent, 'col', 0, 0, tiled=True)  20.7 us
    all_to_all x1, blocking collectives, per_device(): stage = lax.all_to_all(stage, near, 0, 0, tiled=True).reshape(width, width)  15.5 us
    pallas_call x8, Pallas kernels, call(): pl.pallas_call(kernel, out_shape=jax.tree.map(lambda s: jax.ShapeDtypeStr...  13.4 us
    all_to_all x1, blocking collectives, per_device(): slices = lax.all_to_all(corner, near, 0, 0, tiled=True)  11.6 us
    all_to_all x1, starting transfers between devices, per_device(): piece = lax.all_to_all(folded, 'z', 0, 0, tiled=True)  6.43 us
    all_to_all x1, waiting for transfers between devices, per_device(): piece = lax.all_to_all(folded, 'z', 0, 0, tiled=True)  3.33 us
    all_gather x1, blocking collectives, per_device(): lax.all_gather(halves, 'core', axis=0)  2.77 us
  transfers between devices with their start and end apart: 1, of which 1 were waited for; matrix products, arithmetic and copies ran while one was open for 0% of the time, Pallas kernels for 7%

profile of v5, /device:TPU:1, one launch (start us, length us, event | category | flops | bytes accessed | tf_op | source)
XLA Modules:
  0.0 115.6 jit_solution(14088843746642340957)
XLA Ops:
  0.6 0.0 copy-start.3
  0.7 36.7 %all_gather.15 = f32[128,4,256]{2,1,0:T(4,128)S(1)} all-gather(f32[8,4,256]{2,1,0:T(4,128)} %param.6), channel_id=1, replica_groups={{0,48,64,112,128,176,192,240,256,304,320,368,384,432,448,496},{16,32,80..., dimensions={0}, use_global_device_ids=true | all-gather | bytes 557056 | tf_op jit(solution)/shard_map/all_gather | solution.py:135
  37.4 2.2 %all_gather.16 = f32[128,4,256]{2,1,0:T(4,128)S(1)} all-gather(f32[64,4,256]{2,1,0:T(4,128)S(1)} %get-tuple-element.28), channel_id=1, replica_groups=mesh['z'=16,'core'=2,'col'=16] {'core'}, dimensions={0}, use_global_device_ids=true | all-gather | bytes 786432 | tf_op jit(solution)/shard_map/all_gather | solution.py:137
  39.6 2.2 %all_gather.17 = f32[128,4,256]{2,1,0:T(4,128)S(1)} all-gather(f32[64,4,256]{2,1,0:T(4,128)S(1)} %get-tuple-element.16), channel_id=1, replica_groups=mesh['z'=16,'core'=2,'col'=16] {'core'}, dimensions={0}, use_global_device_ids=true | all-gather | bytes 786432 | tf_op jit(solution)/shard_map/all_gather | solution.py:139
  41.7 0.0 copy-done.3
  41.7 0.0 copy-start.2
  41.7 2.2 %shard_map.68 = f32[16,48,256]{2,1,0:T(8,128)S(1)} custom-call(s32[1]{0:T(128)} %bitcast.3.parity_ref, s32[1]{0:T(128)} %bitcast.4.turn_ref, s32[1]{0:T(128)} %bitcast.1.core_ref, f32[4,1024,128]{2,1,0:T(8,128)S(1)} %bitcast.17, f32[2,4,2,8,4,256]{5,4,3,2,1,0:T(4,128)S(1)} %bitcast.13, f32[2,4,2,8,4,256]{5,4,3,2,1,0:T(4,128)S(1)} %bitcast.14), custom_call_target="tpu_custom_call" | custom-call | flops 1600000000 | bytes 4194304 | tf_op jit(solution)/shard_map/pallas_call | solution.py:28
  43.9 0.0 copy-start
  44.0 20.7 %all_to_all.20.got_ref = f32[16,48,256]{2,1,0:T(8,128)S(1)} all-to-all(f32[16,48,256]{2,1,0:T(8,128)S(1)} %shard_map.68), channel_id=1, replica_groups=mesh['z'=16,'core'=2,'col'=16] {'col'}, dimensions={0} | all-to-all | bytes 1572864 | tf_op jit(solution)/shard_map/all_to_all | solution.py:156
  64.7 0.0 copy-done.2
  64.7 2.8 %all-gather = f32[4,16,256]{2,1,0:T(8,128)S(1)} all-gather(f32[2,16,256]{2,1,0:T(8,128)S(1)} %get-tuple-element.23), channel_id=2, replica_groups=mesh['z'=16,'core'=2,'col'=16] {'core'}, dimensions={0}, use_global_device_ids=true | all-gather | bytes 98304 | tf_op jit(solution)/shard_map/all_gather | solution.py:169
  67.5 0.4 shard_map.70
  67.9 11.6 %all_to_all.21.parts_ref = f32[32,8,256]{2,1,0:T(8,128)S(1)} all-to-all(f32[32,8,256]{2,1,0:T(8,128)S(1)} %shard_map.70), channel_id=1, replica_groups=mesh['z'=16,'core'=2,'col'=16] {'core','col'}, dimensions={0} | all-to-all | bytes 524288 | tf_op jit(solution)/shard_map/all_to_all | solution.py:174
  79.5 0.7 shard_map.71
  80.2 6.4 %all-to-all-start.2 = ((f32[16,8,256]{2,1,0:T(8,128)}), f32[16,8,256]{2,1,0:T(8,128)S(1)}, u32[]{:S(2)}, u32[]{:S(2)}) async-start(f32[16,8,256]{2,1,0:T(8,128)} %shard_map.71), calls=%async_computation.2 | async-start | bytes 262144 | tf_op jit(solution)/shard_map/all_to_all | solution.py:178
  86.7 0.0 copy-done
  86.7 0.0 copy-start.1
  86.7 7.6 %shard_map.72.inverse_ref = f32[256,256]{1,0:T(8,128)S(1)} custom-call(f32[256,256]{1,0:T(8,128)S(1)} %copy-done), custom_call_target="tpu_custom_call" | custom-call | flops 3200000000 | bytes 524288 | tf_op jit(solution)/shard_map/pallas_call | solution.py:28
  94.3 0.0 copy-done.1
  94.3 1.0 shard_map.73
  95.3 3.3 %all-to-all-done.2.parts_ref = f32[16,8,256]{2,1,0:T(8,128)S(1)} async-done(((f32[16,8,256]{2,1,0:T(8,128)}), f32[16,8,256]{2,1,0:T(8,128)S(1)}, u32[]{:S(2)}, u32[]{:S(2)}) %all-to-all-start.2) | async-done | bytes 131104 | tf_op jit(solution)/shard_map/all_to_all | solution.py:178
  98.6 0.2 shard_map.74
  98.9 15.5 %all_to_all.22 = f32[32,8,256]{2,1,0:T(8,128)S(1)} all-to-all(f32[32,8,256]{2,1,0:T(8,128)S(1)} %shard_map.74), channel_id=1, replica_groups=mesh['z'=16,'core'=2,'col'=16] {'core','col'}, dimensions={0} | all-to-all | bytes 524288 | tf_op jit(solution)/shard_map/all_to_all | solution.py:202
  114.4 1.2 %shard_map.75 = f32[256,256]{1,0:T(8,128)} custom-call(f32[256,256]{1,0:T(8,128)S(1)} %bitcast.12, f32[256,256]{1,0:T(8,128)S(1)} %shard_map.72.inverse_ref), custom_call_target="tpu_custom_call" | custom-call | tf_op jit(solution)/shard_map/pallas_call | solution.py:28
  (2 shorter events, 0.1 us)
Async XLA Ops:
  0.6 41.1 %copy-start.3 = (f32[4,128,8,128]{3,2,1,0:T(8,128)S(1)}, f32[4,128,8,128]{3,2,1,0:T(8,128)}, u32[]{:S(2)}) copy-start(f32[4,128,8,128]{3,2,1,0:T(8,128)} %param.5) | copy-start | bytes 6291460
  41.7 22.9 %copy-start.2 = (f32[4,8,256]{2,1,0:T(8,128)S(1)}, f32[4,8,256]{2,1,0:T(8,128)}, u32[]{:S(2)}) copy-start(f32[4,8,256]{2,1,0:T(8,128)} %param.7) | copy-start | bytes 98308
  43.9 42.7 %copy-start = (f32[256,256]{1,0:T(8,128)S(1)}, f32[256,256]{1,0:T(8,128)}, u32[]{:S(2)}) copy-start(f32[256,256]{1,0:T(8,128)} %factor_ref.1) | copy-start | bytes 786436
  80.2 18.4 %all-to-all-start.2 = ((f32[16,8,256]{2,1,0:T(8,128)}), f32[16,8,256]{2,1,0:T(8,128)S(1)}, u32[]{:S(2)}, u32[]{:S(2)}) async-start(f32[16,8,256]{2,1,0:T(8,128)} %shard_map.71), calls=%async_computation.2 | async-start | bytes 262144 | tf_op jit(solution)/shard_map/all_to_all | solution.py:178
  86.7 7.6 %copy-start.1 = (f32[256,256]{1,0:T(8,128)S(1)}, f32[256,256]{1,0:T(8,128)}, u32[]{:S(2)}) copy-start(f32[256,256]{1,0:T(8,128)} %adjoint_ref.1) | copy-start | bytes 786436

commit v6 on v5

--- a/solution.py
+++ b/solution.py
@@ -83,14 +83,19 @@
         halves_ref[core] = got_ref[source_ref[0] + core, owned:, :]
 
 
-def corner_kernel(part, core_ref, halves_ref, total_ref, corner_ref, mine_ref):
+def corner_kernel(part, core_ref, turn_ref, halves_ref, total_ref, corner_ref, mine_ref):
     n_core, _, half, _ = halves_ref.shape
     for core in range(n_core):
         rows = halves_ref[core, core_ref[0]]
         for b in range(half // part):
             at = (b * n_core + core) * part
             mine_ref[at:at + part, :] = rows[b * part:(b + 1) * part]
-    corner_ref[...] = dot_tn(mine_ref[...], total_ref[...]).reshape(corner_ref.shape)
+    corner = dot_tn(mine_ref[...], total_ref[...])
+    n_col = corner_ref.shape[0] // n_core
+    for core in range(n_core):
+        held = corner[core * n_col * corner_ref.shape[1]:(core + 1) * n_col * corner_ref.shape[1]]
+        at = (turn_ref[0] ^ core) * n_col
+        corner_ref[pl.ds(at, n_col)] = held.reshape(n_col, *corner_ref.shape[1:])
 
 
 def lower_kernel(total_ref, inverse_ref, adjoint_ref, factor_ref, out_ref, known_ref):
@@ -114,8 +119,9 @@
     out_ref[...] = jnp.broadcast_to(stage[None], out_ref.shape)
 
 
-def finish_kernel(stage_ref, inverse_ref, out_ref):
-    middle = dot_tn(inverse_ref[...], stage_ref[...])
+def finish_kernel(turn_ref, stage_ref, inverse_ref, out_ref):
+    stage = jnp.concatenate([stage_ref[turn_ref[0] ^ core] for core in range(2)], axis=0)
+    middle = dot_tn(inverse_ref[...], stage)
     out_ref[...] = 0.5 * (middle + middle.T)
 
 
@@ -139,13 +145,14 @@
     both = [first, lax.all_gather(rest, "core", axis=0, tiled=True)]
     source = (lax.axis_index("z") * n_core % n_col)[None]
     core = core_at[None]
+    turn = (lax.axis_index("z") % 2)[None]
     adjoint = panel_adj.reshape(row_blocks * share, width)
-    *both, source, core, adjoint = lax.optimization_barrier((*both, source, core, adjoint))
+    *both, source, core, turn, adjoint = lax.optimization_barrier((*both, source, core, turn, adjoint))
     sent = call(
         product_kernel,
         (n_col, row_blocks * (share + part), width),
         (row_at // n_col)[None],
-        (lax.axis_index("z") % 2)[None],
+        turn,
         core,
         gbar.reshape(row_blocks, rows * col_blocks, cols),
         *[b.reshape(n_core, n_z // 4, 2, col_blocks, part, width) for b in both],
@@ -166,16 +173,17 @@
         functools.partial(corner_kernel, part),
         (n_near, count, width),
         core,
+        turn,
         lax.all_gather(halves, "core", axis=0),
         total,
         scratch=[pltpu.VMEM((row_blocks * share, width), F32)],
-        scalars=1,
+        scalars=2,
     )
     slices = lax.all_to_all(corner, near, 0, 0, tiled=True)
     folded, factor = lax.optimization_barrier(
         (call(fold_kernel, (n_z, count, width), slices), factor)
     )
-    piece = lax.all_to_all(folded, "z", 0, 0, tiled=True)
+    piece = lax.all_to_all(folded, ("z", "core"), 0, 0, tiled=True, axis_index_groups=rings)
     inverse = call(
         invert_kernel,
         (width, width),
@@ -193,14 +201,15 @@
     stage = call(
         slice_kernel,
         (n_near, count, width),
-        ((core_at * n_col + col_at) * count)[None],
+        (((core_at ^ turn[0]) * n_col + col_at) * count)[None],
         piece,
         known,
         inverse,
         scalars=1,
     )
-    stage = lax.all_to_all(stage, near, 0, 0, tiled=True).reshape(width, width)
-    corner_adj = call(finish_kernel, (width, width), stage, inverse)
+    stage = lax.all_to_all(stage, near, 0, 0, tiled=True)
+    stage = stage.reshape(n_core, width // n_core, width)
+    corner_adj = call(finish_kernel, (width, width), turn, stage, inverse, scalars=1)
     return lower.reshape(row_blocks, share, width), corner_adj
 
 

time: 116 us -> 116 us (level)
  blocking collectives: 91.6 us -> 89 us
  waiting for transfers between devices: 3.33 us -> 5.52 us
    all_to_all x1, blocking collectives: 15.5 us -> 12.9 us  [per_device(): stage = lax.all_to_all(stage, near, 0, 0, tiled=True)]
    all_to_all x1, waiting for transfers between devices: 3.33 us -> 5.52 us  [per_device(): lax.all_to_all(folded, ('z', 'core'), 0, 0, tiled=True, axis_index_groups...]
where the time goes in v6:
time: 116 us
  blocking collectives  89 us (77%)
  Pallas kernels  13.4 us (12%)
  starting transfers between devices  6.92 us (6%)
  waiting for transfers between devices  5.52 us (5%)
    all_gather x1, blocking collectives, per_device(): lax.all_gather(panel, ('z', 'core'), axis=0, axis_index_groups=rings, til...  36.7 us
    all_to_all x1, blocking collectives, per_device(): got = lax.all_to_all(sent, 'col', 0, 0, tiled=True)  20.7 us
    pallas_call x8, Pallas kernels, call(): pl.pallas_call(kernel, out_shape=jax.tree.map(lambda s: jax.ShapeDtypeStr...  13.4 us
    all_to_all x1, blocking collectives, per_device(): stage = lax.all_to_all(stage, near, 0, 0, tiled=True)  12.9 us
    all_to_all x1, blocking collectives, per_device(): slices = lax.all_to_all(corner, near, 0, 0, tiled=True)  11.6 us
    all_to_all x1, starting transfers between devices, per_device(): lax.all_to_all(folded, ('z', 'core'), 0, 0, tiled=True, axis_index_groups...  6.92 us
    all_to_all x1, waiting for transfers between devices, per_device(): lax.all_to_all(folded, ('z', 'core'), 0, 0, tiled=True, axis_index_groups...  5.52 us
    all_gather x1, blocking collectives, per_device(): lax.all_gather(halves, 'core', axis=0)  2.77 us
  transfers between devices with their start and end apart: 1, of which 1 were waited for; matrix products, arithmetic and copies ran while one was open for 0% of the time, Pallas kernels for 7%

profile of v6, /device:TPU:1, one launch (start us, length us, event | category | flops | bytes accessed | tf_op | source)
XLA Modules:
  0.0 115.6 jit_solution(15468329442627799736)
XLA Ops:
  0.6 0.0 copy-start.3
  0.7 36.7 %all_gather.15 = f32[128,4,256]{2,1,0:T(4,128)S(1)} all-gather(f32[8,4,256]{2,1,0:T(4,128)} %param.6), channel_id=1, replica_groups={{0,48,64,112,128,176,192,240,256,304,320,368,384,432,448,496},{16,32,80..., dimensions={0}, use_global_device_ids=true | all-gather | bytes 557056 | tf_op jit(solution)/shard_map/all_gather | solution.py:141
  37.4 2.2 %all_gather.16 = f32[128,4,256]{2,1,0:T(4,128)S(1)} all-gather(f32[64,4,256]{2,1,0:T(4,128)S(1)} %get-tuple-element.30), channel_id=1, replica_groups=mesh['z'=16,'core'=2,'col'=16] {'core'}, dimensions={0}, use_global_device_ids=true | all-gather | bytes 786432 | tf_op jit(solution)/shard_map/all_gather | solution.py:143
  39.6 2.2 %all_gather.17 = f32[128,4,256]{2,1,0:T(4,128)S(1)} all-gather(f32[64,4,256]{2,1,0:T(4,128)S(1)} %get-tuple-element.17), channel_id=1, replica_groups=mesh['z'=16,'core'=2,'col'=16] {'core'}, dimensions={0}, use_global_device_ids=true | all-gather | bytes 786432 | tf_op jit(solution)/shard_map/all_gather | solution.py:145
  41.7 0.0 copy-done.3
  41.7 0.0 copy-start.2
  41.7 2.2 %shard_map.68 = f32[16,48,256]{2,1,0:T(8,128)S(1)} custom-call(s32[1]{0:T(128)} %bitcast.4.parity_ref, s32[1]{0:T(128)} %bitcast.2.turn_ref, s32[1]{0:T(128)} %bitcast.1.core_ref, f32[4,1024,128]{2,1,0:T(8,128)S(1)} %bitcast.18, f32[2,4,2,8,4,256]{5,4,3,2,1,0:T(4,128)S(1)} %bitcast.14, f32[2,4,2,8,4,256]{5,4,3,2,1,0:T(4,128)S(1)} %bitcast.15), custom_call_target="tpu_custom_call" | custom-call | flops 1600000000 | bytes 4194304 | tf_op jit(solution)/shard_map/pallas_call | solution.py:28
  43.9 0.0 copy-start
  44.0 20.7 %all_to_all.20.got_ref = f32[16,48,256]{2,1,0:T(8,128)S(1)} all-to-all(f32[16,48,256]{2,1,0:T(8,128)S(1)} %shard_map.68), channel_id=1, replica_groups=mesh['z'=16,'core'=2,'col'=16] {'col'}, dimensions={0} | all-to-all | bytes 1572864 | tf_op jit(solution)/shard_map/all_to_all | solution.py:163
  64.7 0.0 copy-done.2
  64.7 2.8 %all-gather = f32[4,16,256]{2,1,0:T(8,128)S(1)} all-gather(f32[2,16,256]{2,1,0:T(8,128)S(1)} %get-tuple-element.25), channel_id=2, replica_groups=mesh['z'=16,'core'=2,'col'=16] {'core'}, dimensions={0}, use_global_device_ids=true | all-gather | bytes 98304 | tf_op jit(solution)/shard_map/all_gather | solution.py:177
  67.5 0.4 shard_map.70
  67.9 11.6 %all_to_all.21.parts_ref = f32[32,8,256]{2,1,0:T(8,128)S(1)} all-to-all(f32[32,8,256]{2,1,0:T(8,128)S(1)} %shard_map.70), channel_id=1, replica_groups=mesh['z'=16,'core'=2,'col'=16] {'core','col'}, dimensions={0} | all-to-all | bytes 524288 | tf_op jit(solution)/shard_map/all_to_all | solution.py:182
  79.5 0.7 shard_map.71
  80.2 6.9 %all-to-all-start.2 = ((f32[16,8,256]{2,1,0:T(8,128)}), f32[16,8,256]{2,1,0:T(8,128)S(1)}, u32[]{:S(2)}, u32[]{:S(2)}) async-start(f32[16,8,256]{2,1,0:T(8,128)} %shard_map.71), calls=%async_computation.2 | async-start | bytes 262144 | tf_op jit(solution)/shard_map/all_to_all | solution.py:186
  87.2 0.0 copy-done
  87.2 0.0 copy-start.1
  87.2 7.6 %shard_map.72.inverse_ref = f32[256,256]{1,0:T(8,128)S(1)} custom-call(f32[256,256]{1,0:T(8,128)S(1)} %copy-done), custom_call_target="tpu_custom_call" | custom-call | flops 3200000000 | bytes 524288 | tf_op jit(solution)/shard_map/pallas_call | solution.py:28
  94.8 0.0 copy-done.1
  94.8 1.0 shard_map.73
  95.8 5.5 %all-to-all-done.2.parts_ref = f32[16,8,256]{2,1,0:T(8,128)S(1)} async-done(((f32[16,8,256]{2,1,0:T(8,128)}), f32[16,8,256]{2,1,0:T(8,128)S(1)}, u32[]{:S(2)}, u32[]{:S(2)}) %all-to-all-start.2) | async-done | bytes 131104 | tf_op jit(solution)/shard_map/all_to_all | solution.py:186
  101.3 0.2 shard_map.74
  101.6 12.9 %all_to_all.22 = f32[32,8,256]{2,1,0:T(8,128)S(1)} all-to-all(f32[32,8,256]{2,1,0:T(8,128)S(1)} %shard_map.74), channel_id=1, replica_groups=mesh['z'=16,'core'=2,'col'=16] {'core','col'}, dimensions={0} | all-to-all | bytes 524288 | tf_op jit(solution)/shard_map/all_to_all | solution.py:210
  114.4 1.2 %shard_map.75 = f32[256,256]{1,0:T(8,128)} custom-call(s32[1]{0:T(128)} %bitcast.2.turn_ref, f32[2,128,256]{2,1,0:T(8,128)S(1)} %bitcast.13, f32[256,256]{1,0:T(8,128)S(1)} %shard_map.72.inverse_ref), custom_call_target="tpu_custom_call" | custom-call | tf_op jit(solution)/shard_map/pallas_call | solution.py:28
  (2 shorter events, 0.1 us)
Async XLA Ops:
  0.6 41.1 %copy-start.3 = (f32[4,128,8,128]{3,2,1,0:T(8,128)S(1)}, f32[4,128,8,128]{3,2,1,0:T(8,128)}, u32[]{:S(2)}) copy-start(f32[4,128,8,128]{3,2,1,0:T(8,128)} %param.5) | copy-start | bytes 6291460
  41.7 22.9 %copy-start.2 = (f32[4,8,256]{2,1,0:T(8,128)S(1)}, f32[4,8,256]{2,1,0:T(8,128)}, u32[]{:S(2)}) copy-start(f32[4,8,256]{2,1,0:T(8,128)} %param.7) | copy-start | bytes 98308
  43.9 43.2 %copy-start = (f32[256,256]{1,0:T(8,128)S(1)}, f32[256,256]{1,0:T(8,128)}, u32[]{:S(2)}) copy-start(f32[256,256]{1,0:T(8,128)} %factor_ref.1) | copy-start | bytes 786436
  80.2 21.1 %all-to-all-start.2 = ((f32[16,8,256]{2,1,0:T(8,128)}), f32[16,8,256]{2,1,0:T(8,128)S(1)}, u32[]{:S(2)}, u32[]{:S(2)}) async-start(f32[16,8,256]{2,1,0:T(8,128)} %shard_map.71), calls=%async_computation.2 | async-start | bytes 262144 | tf_op jit(solution)/shard_map/all_to_all | solution.py:186
  87.2 7.6 %copy-start.1 = (f32[256,256]{1,0:T(8,128)S(1)}, f32[256,256]{1,0:T(8,128)}, u32[]{:S(2)}) copy-start(f32[256,256]{1,0:T(8,128)} %adjoint_ref.1) | copy-start | bytes 786436

commit v7 on v5

--- a/solution.py
+++ b/solution.py
@@ -138,15 +138,15 @@
     rest, first = lax.optimization_barrier((along_z[middle:], first))
     both = [first, lax.all_gather(rest, "core", axis=0, tiled=True)]
     source = (lax.axis_index("z") * n_core % n_col)[None]
-    core = core_at[None]
+    core_here = core_at[None]
     adjoint = panel_adj.reshape(row_blocks * share, width)
-    *both, source, core, adjoint = lax.optimization_barrier((*both, source, core, adjoint))
+    *both, source, core_here, adjoint = lax.optimization_barrier((*both, source, core_here, adjoint))
     sent = call(
         product_kernel,
         (n_col, row_blocks * (share + part), width),
         (row_at // n_col)[None],
         (lax.axis_index("z") % 2)[None],
-        core,
+        core_here,
         gbar.reshape(row_blocks, rows * col_blocks, cols),
         *[b.reshape(n_core, n_z // 4, 2, col_blocks, part, width) for b in both],
         scratch=[pltpu.VMEM((col_blocks, n_z // 2, 2, n_core * part, width), F32)],
@@ -165,7 +165,7 @@
     corner = call(
         functools.partial(corner_kernel, part),
         (n_near, count, width),
-        core,
+        core_here,
         lax.all_gather(halves, "core", axis=0),
         total,
         scratch=[pltpu.VMEM((row_blocks * share, width), F32)],
@@ -175,7 +175,8 @@
     folded, factor = lax.optimization_barrier(
         (call(fold_kernel, (n_z, count, width), slices), factor)
     )
-    piece = lax.all_to_all(folded, "z", 0, 0, tiled=True)
+    lines = [[(z + n_z // 2) % n_z * n_core + core for z in range(n_z)] for core in range(n_core)]
+    piece = lax.all_to_all(folded, ("z", "core"), 0, 0, tiled=True, axis_index_groups=lines)
     inverse = call(
         invert_kernel,
         (width, width),

time: 116 us -> 115 us (level)
  starting transfers between devices: 6.43 us -> 11.5 us
  waiting for transfers between devices: 3.33 us -> 0.01 us
  blocking collectives: 91.6 us -> 89.1 us
    all_to_all x1, starting transfers between devices: 6.43 us -> 11.5 us  [per_device(): lax.all_to_all(folded, ('z', 'core'), 0, 0, tiled=True, axis_index_groups...]
    all_to_all x1, waiting for transfers between devices: 3.33 us -> 0.01 us  [per_device(): lax.all_to_all(folded, ('z', 'core'), 0, 0, tiled=True, axis_index_groups...]
    all_to_all x1, blocking collectives: 15.5 us -> 13 us  [per_device(): stage = lax.all_to_all(stage, near, 0, 0, tiled=True).reshape(width, width)]
  transfers between devices with their start and end apart: 1 -> 1, of which waited for: 1 -> 0; matrix products, arithmetic and copies ran while one was open for 0% -> 0% of each run, Pallas kernels for 7% -> 7%
where the time goes in v7:
time: 115 us
  blocking collectives  89.1 us (77%)
  Pallas kernels  13.4 us (12%)
  starting transfers between devices  11.5 us (10%)
    all_gather x1, blocking collectives, per_device(): lax.all_gather(panel, ('z', 'core'), axis=0, axis_index_groups=rings, til...  36.7 us
    all_to_all x1, blocking collectives, per_device(): got = lax.all_to_all(sent, 'col', 0, 0, tiled=True)  20.7 us
    pallas_call x8, Pallas kernels, call(): pl.pallas_call(kernel, out_shape=jax.tree.map(lambda s: jax.ShapeDtypeStr...  13.4 us
    all_to_all x1, blocking collectives, per_device(): stage = lax.all_to_all(stage, near, 0, 0, tiled=True).reshape(width, width)  13 us
    all_to_all x1, blocking collectives, per_device(): slices = lax.all_to_all(corner, near, 0, 0, tiled=True)  11.6 us
    all_to_all x1, starting transfers between devices, per_device(): lax.all_to_all(folded, ('z', 'core'), 0, 0, tiled=True, axis_index_groups...  11.5 us
    all_gather x1, blocking collectives, per_device(): lax.all_gather(halves, 'core', axis=0)  2.77 us
  transfers between devices with their start and end apart: 1, of which 0 were waited for; matrix products, arithmetic and copies ran while one was open for 0% of the time, Pallas kernels for 7%

profile of v7, /device:TPU:1, one launch (start us, length us, event | category | flops | bytes accessed | tf_op | source)
XLA Modules:
  0.0 114.7 jit_solution(11663547304309718293)
XLA Ops:
  0.6 0.0 copy-start.3
  0.7 36.7 %all_gather.15 = f32[128,4,256]{2,1,0:T(4,128)S(1)} all-gather(f32[8,4,256]{2,1,0:T(4,128)} %param.6), channel_id=1, replica_groups={{0,48,64,112,128,176,192,240,256,304,320,368,384,432,448,496},{16,32,80..., dimensions={0}, use_global_device_ids=true | all-gather | bytes 557056 | tf_op jit(solution)/shard_map/all_gather | solution.py:135
  37.4 2.2 %all_gather.16 = f32[128,4,256]{2,1,0:T(4,128)S(1)} all-gather(f32[64,4,256]{2,1,0:T(4,128)S(1)} %get-tuple-element.28), channel_id=1, replica_groups=mesh['z'=16,'core'=2,'col'=16] {'core'}, dimensions={0}, use_global_device_ids=true | all-gather | bytes 786432 | tf_op jit(solution)/shard_map/all_gather | solution.py:137
  39.6 2.2 %all_gather.17 = f32[128,4,256]{2,1,0:T(4,128)S(1)} all-gather(f32[64,4,256]{2,1,0:T(4,128)S(1)} %get-tuple-element.16), channel_id=1, replica_groups=mesh['z'=16,'core'=2,'col'=16] {'core'}, dimensions={0}, use_global_device_ids=true | all-gather | bytes 786432 | tf_op jit(solution)/shard_map/all_gather | solution.py:139
  41.7 0.0 copy-done.3
  41.7 0.0 copy-start.2
  41.7 2.2 %shard_map.68 = f32[16,48,256]{2,1,0:T(8,128)S(1)} custom-call(s32[1]{0:T(128)} %bitcast.3.parity_ref, s32[1]{0:T(128)} %bitcast.4.turn_ref, s32[1]{0:T(128)} %bitcast.1.core_ref, f32[4,1024,128]{2,1,0:T(8,128)S(1)} %bitcast.17, f32[2,4,2,8,4,256]{5,4,3,2,1,0:T(4,128)S(1)} %bitcast.13, f32[2,4,2,8,4,256]{5,4,3,2,1,0:T(4,128)S(1)} %bitcast.14), custom_call_target="tpu_custom_call" | custom-call | flops 1600000000 | bytes 4194304 | tf_op jit(solution)/shard_map/pallas_call | solution.py:28
  43.9 0.0 copy-start
  44.0 20.7 %all_to_all.20.got_ref = f32[16,48,256]{2,1,0:T(8,128)S(1)} all-to-all(f32[16,48,256]{2,1,0:T(8,128)S(1)} %shard_map.68), channel_id=1, replica_groups=mesh['z'=16,'core'=2,'col'=16] {'col'}, dimensions={0} | all-to-all | bytes 1572864 | tf_op jit(solution)/shard_map/all_to_all | solution.py:156
  64.7 0.0 copy-done.2
  64.7 2.8 %all-gather = f32[4,16,256]{2,1,0:T(8,128)S(1)} all-gather(f32[2,16,256]{2,1,0:T(8,128)S(1)} %get-tuple-element.23), channel_id=2, replica_groups=mesh['z'=16,'core'=2,'col'=16] {'core'}, dimensions={0}, use_global_device_ids=true | all-gather | bytes 98304 | tf_op jit(solution)/shard_map/all_gather | solution.py:169
  67.5 0.4 shard_map.70
  67.9 11.6 %all_to_all.21.parts_ref = f32[32,8,256]{2,1,0:T(8,128)S(1)} all-to-all(f32[32,8,256]{2,1,0:T(8,128)S(1)} %shard_map.70), channel_id=1, replica_groups=mesh['z'=16,'core'=2,'col'=16] {'core','col'}, dimensions={0} | all-to-all | bytes 524288 | tf_op jit(solution)/shard_map/all_to_all | solution.py:174
  79.5 0.7 shard_map.71
  80.2 11.5 %all-to-all-start.2 = ((f32[16,8,256]{2,1,0:T(8,128)}), f32[16,8,256]{2,1,0:T(8,128)S(1)}, u32[]{:S(2)}, u32[]{:S(2)}) async-start(f32[16,8,256]{2,1,0:T(8,128)} %shard_map.71), calls=%async_computation.2 | async-start | bytes 262144 | tf_op jit(solution)/shard_map/all_to_all | solution.py:179
  91.7 0.0 copy-done
  91.7 0.0 copy-start.1
  91.7 7.6 %shard_map.72.inverse_ref = f32[256,256]{1,0:T(8,128)S(1)} custom-call(f32[256,256]{1,0:T(8,128)S(1)} %copy-done), custom_call_target="tpu_custom_call" | custom-call | flops 3200000000 | bytes 524288 | tf_op jit(solution)/shard_map/pallas_call | solution.py:28
  99.3 0.0 copy-done.1
  99.3 1.0 shard_map.73
  100.3 0.0 all-to-all-done.2.parts_ref
  100.3 0.2 shard_map.74
  100.6 13.0 %all_to_all.22 = f32[32,8,256]{2,1,0:T(8,128)S(1)} all-to-all(f32[32,8,256]{2,1,0:T(8,128)S(1)} %shard_map.74), channel_id=1, replica_groups=mesh['z'=16,'core'=2,'col'=16] {'core','col'}, dimensions={0} | all-to-all | bytes 524288 | tf_op jit(solution)/shard_map/all_to_all | solution.py:203
  113.5 1.2 %shard_map.75 = f32[256,256]{1,0:T(8,128)} custom-call(f32[256,256]{1,0:T(8,128)S(1)} %bitcast.12, f32[256,256]{1,0:T(8,128)S(1)} %shard_map.72.inverse_ref), custom_call_target="tpu_custom_call" | custom-call | tf_op jit(solution)/shard_map/pallas_call | solution.py:28
  (2 shorter events, 0.1 us)
Async XLA Ops:
  0.6 41.1 %copy-start.3 = (f32[4,128,8,128]{3,2,1,0:T(8,128)S(1)}, f32[4,128,8,128]{3,2,1,0:T(8,128)}, u32[]{:S(2)}) copy-start(f32[4,128,8,128]{3,2,1,0:T(8,128)} %param.5) | copy-start | bytes 6291460
  41.7 22.9 %copy-start.2 = (f32[4,8,256]{2,1,0:T(8,128)S(1)}, f32[4,8,256]{2,1,0:T(8,128)}, u32[]{:S(2)}) copy-start(f32[4,8,256]{2,1,0:T(8,128)} %param.7) | copy-start | bytes 98308
  43.9 47.7 %copy-start = (f32[256,256]{1,0:T(8,128)S(1)}, f32[256,256]{1,0:T(8,128)}, u32[]{:S(2)}) copy-start(f32[256,256]{1,0:T(8,128)} %factor_ref.1) | copy-start | bytes 786436
  80.2 20.1 %all-to-all-start.2 = ((f32[16,8,256]{2,1,0:T(8,128)}), f32[16,8,256]{2,1,0:T(8,128)S(1)}, u32[]{:S(2)}, u32[]{:S(2)}) async-start(f32[16,8,256]{2,1,0:T(8,128)} %shard_map.71), calls=%async_computation.2 | async-start | bytes 262144 | tf_op jit(solution)/shard_map/all_to_all | solution.py:179
  91.7 7.6 %copy-start.1 = (f32[256,256]{1,0:T(8,128)S(1)}, f32[256,256]{1,0:T(8,128)}, u32[]{:S(2)}) copy-start(f32[256,256]{1,0:T(8,128)} %adjoint_ref.1) | copy-start | bytes 786436

commit v8 on v7

--- a/solution.py
+++ b/solution.py
@@ -35,18 +35,27 @@
     )(*args)
 
 
-def invert_kernel(factor_ref, out_ref):
-    n = factor_ref.shape[0]
+def invert_kernel(factor_ref, adjoint_ref, out_ref, known_ref):
+    n = factor_ref.shape[0] // 2
     i = lax.broadcasted_iota(jnp.int32, (n, n), 0)
     j = lax.broadcasted_iota(jnp.int32, (n, n), 1)
-    lower = factor_ref[...]
-    out_ref[...] = jnp.where(i == j, 1.0 / jnp.where(i == j, lower, 1.0), 0.0)
-    size = 1
+    lowers = [factor_ref[:n, :n], factor_ref[n:, n:]]
+    now = []
+    for lower in lowers:
+        diagonal = jnp.where(i == j, 1.0 / jnp.where(i == j, lower, 1.0), 0.0)
+        scaled = jnp.sum(diagonal, axis=1, keepdims=True) * lower * jnp.sum(diagonal, axis=0, keepdims=True)
+        now.append(diagonal - jnp.where((i == j + 1) & (j % 2 == 0), scaled, 0.0))
+    size = 2
     while size < n:
         below = (i // size == j // size + 1) & (j // size % 2 == 0)
-        now = out_ref[...]
-        out_ref[...] = now - dot(dot(now, jnp.where(below, lower, 0.0)), now)
+        turned = [dot(x, jnp.where(below, lower, 0.0)) for x, lower in zip(now, lowers)]
+        now = [x - dot(t, x) for x, t in zip(now, turned)]
         size *= 2
+    out_ref[:n, :n] = now[0]
+    out_ref[:n, n:] = jnp.zeros((n, n), F32)
+    out_ref[n:, n:] = now[1]
+    out_ref[n:, :n] = -dot(dot(now[1], factor_ref[n:, :n]), now[0])
+    known_ref[...] = dot_tn(adjoint_ref[...], factor_ref[...])
 
 
 def product_kernel(parity_ref, turn_ref, core_ref, gbar_ref, first_ref, second_ref, out_ref, column_ref):
@@ -93,9 +102,8 @@
     corner_ref[...] = dot_tn(mine_ref[...], total_ref[...]).reshape(corner_ref.shape)
 
 
-def lower_kernel(total_ref, inverse_ref, adjoint_ref, factor_ref, out_ref, known_ref):
+def lower_kernel(total_ref, inverse_ref, out_ref):
     out_ref[...] = dot(total_ref[...], inverse_ref[...])
-    known_ref[...] = dot_tn(adjoint_ref[...], factor_ref[...])
 
 
 def fold_kernel(parts_ref, out_ref):
@@ -177,19 +185,12 @@
     )
     lines = [[(z + n_z // 2) % n_z * n_core + core for z in range(n_z)] for core in range(n_core)]
     piece = lax.all_to_all(folded, ("z", "core"), 0, 0, tiled=True, axis_index_groups=lines)
-    inverse = call(
+    inverse, known = call(
         invert_kernel,
-        (width, width),
+        [(width, width), (width, width)],
         factor,
+        factor_adj,
         cost=pl.CostEstimate(flops=int(3.2e9), bytes_accessed=1 << 19, transcendentals=0),
-    )
-    lower, known = call(
-        lower_kernel,
-        [(row_blocks * share, width), (width, width)],
-        total,
-        inverse,
-        factor_adj,
-        factor,
     )
     stage = call(
         slice_kernel,
@@ -199,6 +200,14 @@
         known,
         inverse,
         scalars=1,
+    )
+    total, stage = lax.optimization_barrier((total, stage))
+    lower = call(
+        lower_kernel,
+        (row_blocks * share, width),
+        total,
+        inverse,
+        cost=pl.CostEstimate(flops=int(1e8), bytes_accessed=1 << 19, transcendentals=0),
     )
     stage = lax.all_to_all(stage, near, 0, 0, tiled=True).reshape(width, width)
     corner_adj = call(finish_kernel, (width, width), stage, inverse)

time: 115 us -> 114 us (level)
  blocking collectives: 89.1 us -> 76.1 us
  waiting for transfers between devices: 0.01 us -> 10 us
  starting transfers between devices: 11.5 us -> 17.3 us
  Pallas kernels: 13.4 us -> 9.63 us
    all_to_all x1 -> x0, blocking collectives: 13 us -> none  [per_device(): stage = lax.all_to_all(stage, near, 0, 0, tiled=True).reshape(width, width)]
    all_to_all x0 -> x1, waiting for transfers between devices: none -> 7.45 us  [per_device(): stage = lax.all_to_all(stage, near, 0, 0, tiled=True).reshape(width, width)]
    all_to_all x0 -> x1, starting transfers between devices: none -> 5.84 us  [per_device(): stage = lax.all_to_all(stage, near, 0, 0, tiled=True).reshape(width, width)]
    pallas_call x8, Pallas kernels: 13.4 us -> 9.63 us  [call(): pl.pallas_call(kernel, out_shape=jax.tree.map(lambda s: jax.ShapeDtypeStr...]
    all_to_all x1, waiting for transfers between devices: 0.01 us -> 2.58 us  [per_device(): lax.all_to_all(folded, ('z', 'core'), 0, 0, tiled=True, axis_index_groups...]
  transfers between devices with their start and end apart: 1 -> 2, of which waited for: 0 -> 2; matrix products, arithmetic and copies ran while one was open for 0% -> 0% of each run, Pallas kernels for 7% -> 4%
where the time goes in v8:
time: 114 us
  blocking collectives  76.1 us (67%)
  starting transfers between devices  17.3 us (15%)
  waiting for transfers between devices  10 us (9%)
  Pallas kernels  9.63 us (8%)
    all_gather x1, blocking collectives, per_device(): lax.all_gather(panel, ('z', 'core'), axis=0, axis_index_groups=rings, til...  36.7 us
    all_to_all x1, blocking collectives, per_device(): got = lax.all_to_all(sent, 'col', 0, 0, tiled=True)  20.7 us
    all_to_all x1, blocking collectives, per_device(): slices = lax.all_to_all(corner, near, 0, 0, tiled=True)  11.6 us
    all_to_all x1, starting transfers between devices, per_device(): lax.all_to_all(folded, ('z', 'core'), 0, 0, tiled=True, axis_index_groups...  11.5 us
    pallas_call x8, Pallas kernels, call(): pl.pallas_call(kernel, out_shape=jax.tree.map(lambda s: jax.ShapeDtypeStr...  9.63 us
    all_to_all x1, waiting for transfers between devices, per_device(): stage = lax.all_to_all(stage, near, 0, 0, tiled=True).reshape(width, width)  7.45 us
    all_to_all x1, starting transfers between devices, per_device(): stage = lax.all_to_all(stage, near, 0, 0, tiled=True).reshape(width, width)  5.84 us
    all_gather x1, blocking collectives, per_device(): lax.all_gather(halves, 'core', axis=0)  2.77 us
  transfers between devices with their start and end apart: 2, of which 2 were waited for; matrix products, arithmetic and copies ran while one was open for 0% of the time, Pallas kernels for 4%

profile of v8, /device:TPU:1, one launch (start us, length us, event | category | flops | bytes accessed | tf_op | source)
XLA Modules:
  0.0 113.9 jit_solution(4302777305514610851)
XLA Ops:
  0.6 0.0 copy-start.1
  0.7 36.7 %all_gather.15 = f32[128,4,256]{2,1,0:T(4,128)S(1)} all-gather(f32[8,4,256]{2,1,0:T(4,128)} %param.6), channel_id=1, replica_groups={{0,48,64,112,128,176,192,240,256,304,320,368,384,432,448,496},{16,32,80..., dimensions={0}, use_global_device_ids=true | all-gather | bytes 557056 | tf_op jit(solution)/shard_map/all_gather | solution.py:143
  37.4 2.2 %all_gather.16 = f32[128,4,256]{2,1,0:T(4,128)S(1)} all-gather(f32[64,4,256]{2,1,0:T(4,128)S(1)} %get-tuple-element.32), channel_id=1, replica_groups=mesh['z'=16,'core'=2,'col'=16] {'core'}, dimensions={0}, use_global_device_ids=true | all-gather | bytes 786432 | tf_op jit(solution)/shard_map/all_gather | solution.py:145
  39.6 2.2 %all_gather.17 = f32[128,4,256]{2,1,0:T(4,128)S(1)} all-gather(f32[64,4,256]{2,1,0:T(4,128)S(1)} %get-tuple-element.18), channel_id=1, replica_groups=mesh['z'=16,'core'=2,'col'=16] {'core'}, dimensions={0}, use_global_device_ids=true | all-gather | bytes 786432 | tf_op jit(solution)/shard_map/all_gather | solution.py:147
  41.7 0.0 copy-done.1
  41.7 0.0 copy-start
  41.7 2.2 %shard_map.68 = f32[16,48,256]{2,1,0:T(8,128)S(1)} custom-call(s32[1]{0:T(128)} %bitcast.3.parity_ref, s32[1]{0:T(128)} %bitcast.4.turn_ref, s32[1]{0:T(128)} %bitcast.1.core_ref, f32[4,1024,128]{2,1,0:T(8,128)S(1)} %bitcast.17, f32[2,4,2,8,4,256]{5,4,3,2,1,0:T(4,128)S(1)} %bitcast.13, f32[2,4,2,8,4,256]{5,4,3,2,1,0:T(4,128)S(1)} %bitcast.14), custom_call_target="tpu_custom_call" | custom-call | flops 1600000000 | bytes 4194304 | tf_op jit(solution)/shard_map/pallas_call | solution.py:28
  43.9 0.0 copy-start.2
  44.0 0.0 copy-start.3
  44.0 20.7 %all_to_all.20.got_ref = f32[16,48,256]{2,1,0:T(8,128)S(1)} all-to-all(f32[16,48,256]{2,1,0:T(8,128)S(1)} %shard_map.68), channel_id=1, replica_groups=mesh['z'=16,'core'=2,'col'=16] {'col'}, dimensions={0} | all-to-all | bytes 1572864 | tf_op jit(solution)/shard_map/all_to_all | solution.py:164
  64.7 0.0 copy-done
  64.7 2.8 %all-gather = f32[4,16,256]{2,1,0:T(8,128)S(1)} all-gather(f32[2,16,256]{2,1,0:T(8,128)S(1)} %get-tuple-element.25), channel_id=2, replica_groups=mesh['z'=16,'core'=2,'col'=16] {'core'}, dimensions={0}, use_global_device_ids=true | all-gather | bytes 98304 | tf_op jit(solution)/shard_map/all_gather | solution.py:177
  67.5 0.4 shard_map.70
  67.9 11.6 %all_to_all.21.parts_ref = f32[32,8,256]{2,1,0:T(8,128)S(1)} all-to-all(f32[32,8,256]{2,1,0:T(8,128)S(1)} %shard_map.70), channel_id=1, replica_groups=mesh['z'=16,'core'=2,'col'=16] {'core','col'}, dimensions={0} | all-to-all | bytes 524288 | tf_op jit(solution)/shard_map/all_to_all | solution.py:182
  79.5 0.7 shard_map.71
  80.2 11.5 %all-to-all-start.2 = ((f32[16,8,256]{2,1,0:T(8,128)}), f32[16,8,256]{2,1,0:T(8,128)S(1)}, u32[]{:S(2)}, u32[]{:S(2)}) async-start(f32[16,8,256]{2,1,0:T(8,128)} %shard_map.71), calls=%async_computation.2 | async-start | bytes 262144 | tf_op jit(solution)/shard_map/all_to_all | solution.py:187
  91.7 0.0 copy-done.2
  91.7 0.0 copy-done.3
  91.7 3.3 %shard_map.72 = (f32[256,256]{1,0:T(8,128)S(1)}, f32[256,256]{1,0:T(8,128)S(1)}) custom-call(f32[256,256]{1,0:T(8,128)S(1)} %copy-done.2, f32[256,256]{1,0:T(8,128)S(1)} %copy-done.3), custom_call_target="tpu_custom_call" | custom-call | flops 3200000000 | bytes 524288 | tf_op jit(solution)/shard_map/pallas_call | solution.py:28
  95.0 2.6 %all-to-all-done.2.parts_ref = f32[16,8,256]{2,1,0:T(8,128)S(1)} async-done(((f32[16,8,256]{2,1,0:T(8,128)}), f32[16,8,256]{2,1,0:T(8,128)S(1)}, u32[]{:S(2)}, u32[]{:S(2)}) %all-to-all-start.2) | async-done | bytes 131104 | tf_op jit(solution)/shard_map/all_to_all | solution.py:187
  97.6 1.0 shard_map.73
  98.5 5.8 %all-to-all-start.3 = ((f32[32,8,256]{2,1,0:T(8,128)}), f32[32,8,256]{2,1,0:T(8,128)S(1)}, u32[]{:S(2)}, u32[]{:S(2)}) async-start(f32[32,8,256]{2,1,0:T(8,128)} %shard_map.73), calls=%async_computation.3 | async-start | bytes 524288 | tf_op jit(solution)/shard_map/all_to_all | solution.py:212
  104.4 0.8 shard_map.74
  105.2 7.4 %all-to-all-done.3 = f32[32,8,256]{2,1,0:T(8,128)S(1)} async-done(((f32[32,8,256]{2,1,0:T(8,128)}), f32[32,8,256]{2,1,0:T(8,128)S(1)}, u32[]{:S(2)}, u32[]{:S(2)}) %all-to-all-start.3) | async-done | bytes 262176 | tf_op jit(solution)/shard_map/all_to_all | solution.py:212
  112.7 1.2 %shard_map.75 = f32[256,256]{1,0:T(8,128)} custom-call(f32[256,256]{1,0:T(8,128)S(1)} %bitcast.12, f32[256,256]{1,0:T(8,128)S(1)} %get-tuple-element.29.inverse_ref), custom_call_target="tpu_custom_call" | custom-call | tf_op jit(solution)/shard_map/pallas_call | solution.py:28
  (2 shorter events, 0.1 us)
Async XLA Ops:
  0.6 41.1 %copy-start.1 = (f32[4,128,8,128]{3,2,1,0:T(8,128)S(1)}, f32[4,128,8,128]{3,2,1,0:T(8,128)}, u32[]{:S(2)}) copy-start(f32[4,128,8,128]{3,2,1,0:T(8,128)} %param.5) | copy-start | bytes 6291460
  41.7 23.0 %copy-start = (f32[4,8,256]{2,1,0:T(8,128)S(1)}, f32[4,8,256]{2,1,0:T(8,128)}, u32[]{:S(2)}) copy-start(f32[4,8,256]{2,1,0:T(8,128)} %param.7) | copy-start | bytes 98308
  43.9 47.8 %copy-start.2 = (f32[256,256]{1,0:T(8,128)S(1)}, f32[256,256]{1,0:T(8,128)}, u32[]{:S(2)}) copy-start(f32[256,256]{1,0:T(8,128)} %factor_ref) | copy-start | bytes 786436
  44.0 47.8 %copy-start.3 = (f32[256,256]{1,0:T(8,128)S(1)}, f32[256,256]{1,0:T(8,128)}, u32[]{:S(2)}) copy-start(f32[256,256]{1,0:T(8,128)} %adjoint_ref.1) | copy-start | bytes 786436
  80.2 17.3 %all-to-all-start.2 = ((f32[16,8,256]{2,1,0:T(8,128)}), f32[16,8,256]{2,1,0:T(8,128)S(1)}, u32[]{:S(2)}, u32[]{:S(2)}) async-start(f32[16,8,256]{2,1,0:T(8,128)} %shard_map.71), calls=%async_computation.2 | async-start | bytes 262144 | tf_op jit(solution)/shard_map/all_to_all | solution.py:187
  98.5 14.1 %all-to-all-start.3 = ((f32[32,8,256]{2,1,0:T(8,128)}), f32[32,8,256]{2,1,0:T(8,128)S(1)}, u32[]{:S(2)}, u32[]{:S(2)}) async-start(f32[32,8,256]{2,1,0:T(8,128)} %shard_map.73), calls=%async_computation.3 | async-start | bytes 524288 | tf_op jit(solution)/shard_map/all_to_all | solution.py:212

commit v9 on v8

--- a/solution.py
+++ b/solution.py
@@ -192,6 +192,14 @@
         factor_adj,
         cost=pl.CostEstimate(flops=int(3.2e9), bytes_accessed=1 << 19, transcendentals=0),
     )
+    lower = call(
+        lower_kernel,
+        (row_blocks * share, width),
+        total,
+        inverse,
+        cost=pl.CostEstimate(flops=int(1e8), bytes_accessed=1 << 19, transcendentals=0),
+    )
+    known, lower = lax.optimization_barrier((known, lower))
     stage = call(
         slice_kernel,
         (n_near, count, width),
@@ -200,14 +208,6 @@
         known,
         inverse,
         scalars=1,
-    )
-    total, stage = lax.optimization_barrier((total, stage))
-    lower = call(
-        lower_kernel,
-        (row_blocks * share, width),
-        total,
-        inverse,
-        cost=pl.CostEstimate(flops=int(1e8), bytes_accessed=1 << 19, transcendentals=0),
     )
     stage = lax.all_to_all(stage, near, 0, 0, tiled=True).reshape(width, width)
     corner_adj = call(finish_kernel, (width, width), stage, inverse)

time: 114 us -> 113 us (level)
  blocking collectives: 76.1 us -> 90.1 us
  waiting for transfers between devices: 10 us -> 1.73 us
  starting transfers between devices: 17.3 us -> 11.5 us
    all_to_all x0 -> x1, blocking collectives: none -> 13.9 us  [per_device(): stage = lax.all_to_all(stage, near, 0, 0, tiled=True).reshape(width, width)]
    all_to_all x1 -> x0, waiting for transfers between devices: 7.45 us -> none  [per_device(): stage = lax.all_to_all(stage, near, 0, 0, tiled=True).reshape(width, width)]
    all_to_all x1 -> x0, starting transfers between devices: 5.84 us -> none  [per_device(): stage = lax.all_to_all(stage, near, 0, 0, tiled=True).reshape(width, width)]
  transfers between devices with their start and end apart: 2 -> 1, of which waited for: 2 -> 1; matrix products, arithmetic and copies ran while one was open for 0% -> 0% of each run, Pallas kernels for 4% -> 4%
where the time goes in v9:
time: 113 us
  blocking collectives  90.1 us (80%)
  starting transfers between devices  11.5 us (10%)
  Pallas kernels  8.92 us (8%)
  waiting for transfers between devices  1.73 us (2%)
    all_gather x1, blocking collectives, per_device(): lax.all_gather(panel, ('z', 'core'), axis=0, axis_index_groups=rings, til...  36.7 us
    all_to_all x1, blocking collectives, per_device(): got = lax.all_to_all(sent, 'col', 0, 0, tiled=True)  20.7 us
    all_to_all x1, blocking collectives, per_device(): stage = lax.all_to_all(stage, near, 0, 0, tiled=True).reshape(width, width)  13.9 us
    all_to_all x1, blocking collectives, per_device(): slices = lax.all_to_all(corner, near, 0, 0, tiled=True)  11.6 us
    all_to_all x1, starting transfers between devices, per_device(): lax.all_to_all(folded, ('z', 'core'), 0, 0, tiled=True, axis_index_groups...  11.5 us
    pallas_call x8, Pallas kernels, call(): pl.pallas_call(kernel, out_shape=jax.tree.map(lambda s: jax.ShapeDtypeStr...  8.92 us
    all_gather x1, blocking collectives, per_device(): lax.all_gather(halves, 'core', axis=0)  2.77 us
  transfers between devices with their start and end apart: 1, of which 1 were waited for; matrix products, arithmetic and copies ran while one was open for 0% of the time, Pallas kernels for 4%

profile of v9, /device:TPU:1, one launch (start us, length us, event | category | flops | bytes accessed | tf_op | source)
XLA Modules:
  0.0 113.0 jit_solution(14843009715326205449)
XLA Ops:
  0.6 0.0 copy-start.1
  0.7 36.7 %all_gather.15 = f32[128,4,256]{2,1,0:T(4,128)S(1)} all-gather(f32[8,4,256]{2,1,0:T(4,128)} %param.6), channel_id=1, replica_groups={{0,48,64,112,128,176,192,240,256,304,320,368,384,432,448,496},{16,32,80..., dimensions={0}, use_global_device_ids=true | all-gather | bytes 557056 | tf_op jit(solution)/shard_map/all_gather | solution.py:143
  37.4 2.2 %all_gather.16 = f32[128,4,256]{2,1,0:T(4,128)S(1)} all-gather(f32[64,4,256]{2,1,0:T(4,128)S(1)} %get-tuple-element.32), channel_id=1, replica_groups=mesh['z'=16,'core'=2,'col'=16] {'core'}, dimensions={0}, use_global_device_ids=true | all-gather | bytes 786432 | tf_op jit(solution)/shard_map/all_gather | solution.py:145
  39.6 2.2 %all_gather.17 = f32[128,4,256]{2,1,0:T(4,128)S(1)} all-gather(f32[64,4,256]{2,1,0:T(4,128)S(1)} %get-tuple-element.18), channel_id=1, replica_groups=mesh['z'=16,'core'=2,'col'=16] {'core'}, dimensions={0}, use_global_device_ids=true | all-gather | bytes 786432 | tf_op jit(solution)/shard_map/all_gather | solution.py:147
  41.7 0.0 copy-done.1
  41.7 0.0 copy-start
  41.7 2.2 %shard_map.68 = f32[16,48,256]{2,1,0:T(8,128)S(1)} custom-call(s32[1]{0:T(128)} %bitcast.3.parity_ref, s32[1]{0:T(128)} %bitcast.4.turn_ref, s32[1]{0:T(128)} %bitcast.1.core_ref, f32[4,1024,128]{2,1,0:T(8,128)S(1)} %bitcast.17, f32[2,4,2,8,4,256]{5,4,3,2,1,0:T(4,128)S(1)} %bitcast.13, f32[2,4,2,8,4,256]{5,4,3,2,1,0:T(4,128)S(1)} %bitcast.14), custom_call_target="tpu_custom_call" | custom-call | flops 1600000000 | bytes 4194304 | tf_op jit(solution)/shard_map/pallas_call | solution.py:28
  43.9 0.0 copy-start.2
  44.0 0.0 copy-start.3
  44.0 20.7 %all_to_all.20.got_ref = f32[16,48,256]{2,1,0:T(8,128)S(1)} all-to-all(f32[16,48,256]{2,1,0:T(8,128)S(1)} %shard_map.68), channel_id=1, replica_groups=mesh['z'=16,'core'=2,'col'=16] {'col'}, dimensions={0} | all-to-all | bytes 1572864 | tf_op jit(solution)/shard_map/all_to_all | solution.py:164
  64.7 0.0 copy-done
  64.7 2.8 %all-gather = f32[4,16,256]{2,1,0:T(8,128)S(1)} all-gather(f32[2,16,256]{2,1,0:T(8,128)S(1)} %get-tuple-element.24), channel_id=2, replica_groups=mesh['z'=16,'core'=2,'col'=16] {'core'}, dimensions={0}, use_global_device_ids=true | all-gather | bytes 98304 | tf_op jit(solution)/shard_map/all_gather | solution.py:177
  67.5 0.4 shard_map.70
  67.9 11.6 %all_to_all.21.parts_ref = f32[32,8,256]{2,1,0:T(8,128)S(1)} all-to-all(f32[32,8,256]{2,1,0:T(8,128)S(1)} %shard_map.70), channel_id=1, replica_groups=mesh['z'=16,'core'=2,'col'=16] {'core','col'}, dimensions={0} | all-to-all | bytes 524288 | tf_op jit(solution)/shard_map/all_to_all | solution.py:182
  79.5 0.7 shard_map.71
  80.2 11.5 %all-to-all-start.2 = ((f32[16,8,256]{2,1,0:T(8,128)}), f32[16,8,256]{2,1,0:T(8,128)S(1)}, u32[]{:S(2)}, u32[]{:S(2)}) async-start(f32[16,8,256]{2,1,0:T(8,128)} %shard_map.71), calls=%async_computation.2 | async-start | bytes 262144 | tf_op jit(solution)/shard_map/all_to_all | solution.py:187
  91.7 0.0 copy-done.2
  91.7 0.0 copy-done.3
  91.7 3.3 %shard_map.72 = (f32[256,256]{1,0:T(8,128)S(1)}, f32[256,256]{1,0:T(8,128)S(1)}) custom-call(f32[256,256]{1,0:T(8,128)S(1)} %copy-done.2, f32[256,256]{1,0:T(8,128)S(1)} %copy-done.3), custom_call_target="tpu_custom_call" | custom-call | flops 3200000000 | bytes 524288 | tf_op jit(solution)/shard_map/pallas_call | solution.py:28
  95.0 0.8 shard_map.73
  95.9 1.7 %all-to-all-done.2.parts_ref = f32[16,8,256]{2,1,0:T(8,128)S(1)} async-done(((f32[16,8,256]{2,1,0:T(8,128)}), f32[16,8,256]{2,1,0:T(8,128)S(1)}, u32[]{:S(2)}, u32[]{:S(2)}) %all-to-all-start.2) | async-done | bytes 131104 | tf_op jit(solution)/shard_map/all_to_all | solution.py:187
  97.6 0.2 shard_map.74
  97.8 13.9 %all_to_all.22 = f32[32,8,256]{2,1,0:T(8,128)S(1)} all-to-all(f32[32,8,256]{2,1,0:T(8,128)S(1)} %shard_map.74), channel_id=1, replica_groups=mesh['z'=16,'core'=2,'col'=16] {'core','col'}, dimensions={0} | all-to-all | bytes 524288 | tf_op jit(solution)/shard_map/all_to_all | solution.py:212
  111.8 1.2 %shard_map.75 = f32[256,256]{1,0:T(8,128)} custom-call(f32[256,256]{1,0:T(8,128)S(1)} %bitcast.12, f32[256,256]{1,0:T(8,128)S(1)} %get-tuple-element.28.inverse_ref), custom_call_target="tpu_custom_call" | custom-call | tf_op jit(solution)/shard_map/pallas_call | solution.py:28
  (2 shorter events, 0.1 us)
Async XLA Ops:
  0.6 41.1 %copy-start.1 = (f32[4,128,8,128]{3,2,1,0:T(8,128)S(1)}, f32[4,128,8,128]{3,2,1,0:T(8,128)}, u32[]{:S(2)}) copy-start(f32[4,128,8,128]{3,2,1,0:T(8,128)} %param.5) | copy-start | bytes 6291460
  41.7 23.0 %copy-start = (f32[4,8,256]{2,1,0:T(8,128)S(1)}, f32[4,8,256]{2,1,0:T(8,128)}, u32[]{:S(2)}) copy-start(f32[4,8,256]{2,1,0:T(8,128)} %param.7) | copy-start | bytes 98308
  43.9 47.8 %copy-start.2 = (f32[256,256]{1,0:T(8,128)S(1)}, f32[256,256]{1,0:T(8,128)}, u32[]{:S(2)}) copy-start(f32[256,256]{1,0:T(8,128)} %factor_ref) | copy-start | bytes 786436
  44.0 47.8 %copy-start.3 = (f32[256,256]{1,0:T(8,128)S(1)}, f32[256,256]{1,0:T(8,128)}, u32[]{:S(2)}) copy-start(f32[256,256]{1,0:T(8,128)} %adjoint_ref.1) | copy-start | bytes 786436
  80.2 17.3 %all-to-all-start.2 = ((f32[16,8,256]{2,1,0:T(8,128)}), f32[16,8,256]{2,1,0:T(8,128)S(1)}, u32[]{:S(2)}, u32[]{:S(2)}) async-start(f32[16,8,256]{2,1,0:T(8,128)} %shard_map.71), calls=%async_computation.2 | async-start | bytes 262144 | tf_op jit(solution)/shard_map/all_to_all | solution.py:187

commit v10 on v9

--- a/solution.py
+++ b/solution.py
@@ -35,7 +35,7 @@
     )(*args)
 
 
-def invert_kernel(factor_ref, adjoint_ref, out_ref, known_ref):
+def invert_kernel(factor_ref, adjoint_ref, out_ref, flipped_ref, known_ref):
     n = factor_ref.shape[0] // 2
     i = lax.broadcasted_iota(jnp.int32, (n, n), 0)
     j = lax.broadcasted_iota(jnp.int32, (n, n), 1)
@@ -55,6 +55,7 @@
     out_ref[:n, n:] = jnp.zeros((n, n), F32)
     out_ref[n:, n:] = now[1]
     out_ref[n:, :n] = -dot(dot(now[1], factor_ref[n:, :n]), now[0])
+    flipped_ref[...] = out_ref[...].T
     known_ref[...] = dot_tn(adjoint_ref[...], factor_ref[...])
 
 
@@ -122,8 +123,8 @@
     out_ref[...] = jnp.broadcast_to(stage[None], out_ref.shape)
 
 
-def finish_kernel(stage_ref, inverse_ref, out_ref):
-    middle = dot_tn(inverse_ref[...], stage_ref[...])
+def finish_kernel(stage_ref, flipped_ref, out_ref):
+    middle = dot(flipped_ref[...], stage_ref[...])
     out_ref[...] = 0.5 * (middle + middle.T)
 
 
@@ -185,9 +186,9 @@
     )
     lines = [[(z + n_z // 2) % n_z * n_core + core for z in range(n_z)] for core in range(n_core)]
     piece = lax.all_to_all(folded, ("z", "core"), 0, 0, tiled=True, axis_index_groups=lines)
-    inverse, known = call(
+    inverse, flipped, known = call(
         invert_kernel,
-        [(width, width), (width, width)],
+        [(width, width)] * 3,
         factor,
         factor_adj,
         cost=pl.CostEstimate(flops=int(3.2e9), bytes_accessed=1 << 19, transcendentals=0),
@@ -202,15 +203,16 @@
     known, lower = lax.optimization_barrier((known, lower))
     stage = call(
         slice_kernel,
-        (n_near, count, width),
+        (n_col, count, width),
         ((core_at * n_col + col_at) * count)[None],
         piece,
         known,
         inverse,
         scalars=1,
     )
-    stage = lax.all_to_all(stage, near, 0, 0, tiled=True).reshape(width, width)
-    corner_adj = call(finish_kernel, (width, width), stage, inverse)
+    stage = lax.all_to_all(stage, "col", 0, 0, tiled=True)
+    stage = lax.all_gather(stage, "core", axis=0).reshape(width, width)
+    corner_adj = call(finish_kernel, (width, width), stage, flipped)
     return lower.reshape(row_blocks, share, width), corner_adj
 
 

time: 113 us -> 115 us (1.018)
  blocking collectives: 90.1 us -> 91.3 us
    all_gather x0 -> x1, blocking collectives: none -> 3.93 us  [per_device(): stage = lax.all_gather(stage, 'core', axis=0).reshape(width, width)]
    all_to_all x1, blocking collectives: 13.9 us -> 11.3 us  [per_device(): stage = lax.all_to_all(stage, 'col', 0, 0, tiled=True)]
where the time goes in v10:
time: 115 us; the launch traced here: 114 us
  blocking collectives  91.3 us (79%)
  starting transfers between devices  11.5 us (10%)
  Pallas kernels  8.87 us (8%)
  waiting for transfers between devices  1.73 us (2%)
    all_gather x1, blocking collectives, per_device(): lax.all_gather(panel, ('z', 'core'), axis=0, axis_index_groups=rings, til...  36.7 us
    all_to_all x1, blocking collectives, per_device(): got = lax.all_to_all(sent, 'col', 0, 0, tiled=True)  20.7 us
    all_to_all x1, blocking collectives, per_device(): slices = lax.all_to_all(corner, near, 0, 0, tiled=True)  11.6 us
    all_to_all x1, starting transfers between devices, per_device(): lax.all_to_all(folded, ('z', 'core'), 0, 0, tiled=True, axis_index_groups...  11.5 us
    all_to_all x1, blocking collectives, per_device(): stage = lax.all_to_all(stage, 'col', 0, 0, tiled=True)  11.3 us
    pallas_call x8, Pallas kernels, call(): pl.pallas_call(kernel, out_shape=jax.tree.map(lambda s: jax.ShapeDtypeStr...  8.87 us
    all_gather x1, blocking collectives, per_device(): stage = lax.all_gather(stage, 'core', axis=0).reshape(width, width)  3.93 us
    all_gather x1, blocking collectives, per_device(): lax.all_gather(halves, 'core', axis=0)  2.77 us
  transfers between devices with their start and end apart: 1, of which 1 were waited for; matrix products, arithmetic and copies ran while one was open for 0% of the time, Pallas kernels for 4%

profile of v10, /device:TPU:1, one launch (start us, length us, event | category | flops | bytes accessed | tf_op | source)
XLA Modules:
  0.0 114.2 jit_solution(650189733672338734)
XLA Ops:
  0.6 0.0 copy-start.1
  0.7 36.7 %all_gather.21 = f32[128,4,256]{2,1,0:T(4,128)S(1)} all-gather(f32[8,4,256]{2,1,0:T(4,128)} %param.6), channel_id=1, replica_groups={{0,48,64,112,128,176,192,240,256,304,320,368,384,432,448,496},{16,32,80..., dimensions={0}, use_global_device_ids=true | all-gather | bytes 557056 | tf_op jit(solution)/shard_map/all_gather | solution.py:144
  37.4 2.2 %all_gather.22 = f32[128,4,256]{2,1,0:T(4,128)S(1)} all-gather(f32[64,4,256]{2,1,0:T(4,128)S(1)} %get-tuple-element.34), channel_id=1, replica_groups=mesh['z'=16,'core'=2,'col'=16] {'core'}, dimensions={0}, use_global_device_ids=true | all-gather | bytes 786432 | tf_op jit(solution)/shard_map/all_gather | solution.py:146
  39.6 2.2 %all_gather.23 = f32[128,4,256]{2,1,0:T(4,128)S(1)} all-gather(f32[64,4,256]{2,1,0:T(4,128)S(1)} %get-tuple-element.19), channel_id=1, replica_groups=mesh['z'=16,'core'=2,'col'=16] {'core'}, dimensions={0}, use_global_device_ids=true | all-gather | bytes 786432 | tf_op jit(solution)/shard_map/all_gather | solution.py:148
  41.7 0.0 copy-done.1
  41.7 0.0 copy-start
  41.7 2.2 %shard_map.68 = f32[16,48,256]{2,1,0:T(8,128)S(1)} custom-call(s32[1]{0:T(128)} %bitcast.3.parity_ref, s32[1]{0:T(128)} %bitcast.4.turn_ref, s32[1]{0:T(128)} %bitcast.1.core_ref, f32[4,1024,128]{2,1,0:T(8,128)S(1)} %bitcast.17, f32[2,4,2,8,4,256]{5,4,3,2,1,0:T(4,128)S(1)} %bitcast.13, f32[2,4,2,8,4,256]{5,4,3,2,1,0:T(4,128)S(1)} %bitcast.14), custom_call_target="tpu_custom_call" | custom-call | flops 1600000000 | bytes 4194304 | tf_op jit(solution)/shard_map/pallas_call | solution.py:28
  43.9 0.0 copy-start.2
  44.0 0.0 copy-start.3
  44.0 20.7 %all_to_all.20.got_ref = f32[16,48,256]{2,1,0:T(8,128)S(1)} all-to-all(f32[16,48,256]{2,1,0:T(8,128)S(1)} %shard_map.68), channel_id=1, replica_groups=mesh['z'=16,'core'=2,'col'=16] {'col'}, dimensions={0} | all-to-all | bytes 1572864 | tf_op jit(solution)/shard_map/all_to_all | solution.py:165
  64.7 0.0 copy-done
  64.7 2.8 %all-gather = f32[4,16,256]{2,1,0:T(8,128)S(1)} all-gather(f32[2,16,256]{2,1,0:T(8,128)S(1)} %get-tuple-element.25), channel_id=2, replica_groups=mesh['z'=16,'core'=2,'col'=16] {'core'}, dimensions={0}, use_global_device_ids=true | all-gather | bytes 98304 | tf_op jit(solution)/shard_map/all_gather | solution.py:178
  67.5 0.4 shard_map.70
  67.9 11.6 %all_to_all.21.parts_ref = f32[32,8,256]{2,1,0:T(8,128)S(1)} all-to-all(f32[32,8,256]{2,1,0:T(8,128)S(1)} %shard_map.70), channel_id=1, replica_groups=mesh['z'=16,'core'=2,'col'=16] {'core','col'}, dimensions={0} | all-to-all | bytes 524288 | tf_op jit(solution)/shard_map/all_to_all | solution.py:183
  79.5 0.7 shard_map.71
  80.2 11.5 %all-to-all-start.2 = ((f32[16,8,256]{2,1,0:T(8,128)}), f32[16,8,256]{2,1,0:T(8,128)S(1)}, u32[]{:S(2)}, u32[]{:S(2)}) async-start(f32[16,8,256]{2,1,0:T(8,128)} %shard_map.71), calls=%async_computation.2 | async-start | bytes 262144 | tf_op jit(solution)/shard_map/all_to_all | solution.py:188
  91.7 0.0 copy-done.2
  91.7 0.0 copy-done.3
  91.7 3.3 %shard_map.72 = (f32[256,256]{1,0:T(8,128)S(1)}, f32[256,256]{1,0:T(8,128)S(1)}, f32[256,256]{1,0:T(8,128)S(1)}) custom-call(f32[256,256]{1,0:T(8,128)S(1)} %copy-done.2, f32[256,256]{1,0:T(8,128)S(1)} %copy-done.3), custom_call_target="tpu_custom_call" | custom-call | flops 3200000000 | bytes 524288 | tf_op jit(solution)/shard_map/pallas_call | solution.py:28
  95.0 0.8 shard_map.73
  95.9 1.7 %all-to-all-done.2.parts_ref = f32[16,8,256]{2,1,0:T(8,128)S(1)} async-done(((f32[16,8,256]{2,1,0:T(8,128)}), f32[16,8,256]{2,1,0:T(8,128)S(1)}, u32[]{:S(2)}, u32[]{:S(2)}) %all-to-all-start.2) | async-done | bytes 131104 | tf_op jit(solution)/shard_map/all_to_all | solution.py:188
  97.6 0.2 shard_map.74
  97.8 11.3 %all_to_all.22 = f32[16,8,256]{2,1,0:T(8,128)S(1)} all-to-all(f32[16,8,256]{2,1,0:T(8,128)S(1)} %shard_map.74), channel_id=1, replica_groups=mesh['z'=16,'core'=2,'col'=16] {'col'}, dimensions={0} | all-to-all | bytes 262144 | tf_op jit(solution)/shard_map/all_to_all | solution.py:213
  109.1 3.9 %all-gather.1 = f32[32,8,256]{2,1,0:T(8,128)S(1)} all-gather(f32[16,8,256]{2,1,0:T(8,128)S(1)} %all_to_all.22), channel_id=3, replica_groups=mesh['z'=16,'core'=2,'col'=16] {'core'}, dimensions={0}, use_global_device_ids=true | all-gather | bytes 393216 | tf_op jit(solution)/shard_map/all_gather | solution.py:214
  113.0 1.2 %shard_map.75 = f32[256,256]{1,0:T(8,128)} custom-call(f32[256,256]{1,0:T(8,128)S(1)} %bitcast.12, f32[256,256]{1,0:T(8,128)S(1)} %get-tuple-element.33.flipped_ref), custom_call_target="tpu_custom_call" | custom-call | tf_op jit(solution)/shard_map/pallas_call | solution.py:28
  (2 shorter events, 0.1 us)
Async XLA Ops:
  0.6 41.1 %copy-start.1 = (f32[4,128,8,128]{3,2,1,0:T(8,128)S(1)}, f32[4,128,8,128]{3,2,1,0:T(8,128)}, u32[]{:S(2)}) copy-start(f32[4,128,8,128]{3,2,1,0:T(8,128)} %param.5) | copy-start | bytes 6291460
  41.7 23.0 %copy-start = (f32[4,8,256]{2,1,0:T(8,128)S(1)}, f32[4,8,256]{2,1,0:T(8,128)}, u32[]{:S(2)}) copy-start(f32[4,8,256]{2,1,0:T(8,128)} %param.7) | copy-start | bytes 98308
  43.9 47.8 %copy-start.2 = (f32[256,256]{1,0:T(8,128)S(1)}, f32[256,256]{1,0:T(8,128)}, u32[]{:S(2)}) copy-start(f32[256,256]{1,0:T(8,128)} %factor_ref) | copy-start | bytes 786436
  44.0 47.8 %copy-start.3 = (f32[256,256]{1,0:T(8,128)S(1)}, f32[256,256]{1,0:T(8,128)}, u32[]{:S(2)}) copy-start(f32[256,256]{1,0:T(8,128)} %adjoint_ref.1) | copy-start | bytes 786436
  80.2 17.3 %all-to-all-start.2 = ((f32[16,8,256]{2,1,0:T(8,128)}), f32[16,8,256]{2,1,0:T(8,128)S(1)}, u32[]{:S(2)}, u32[]{:S(2)}) async-start(f32[16,8,256]{2,1,0:T(8,128)} %shard_map.71), calls=%async_computation.2 | async-start | bytes 262144 | tf_op jit(solution)/shard_map/all_to_all | solution.py:188

commit v11 on v9

--- a/solution.py
+++ b/solution.py
@@ -73,11 +73,13 @@
                     held = from_ref[turn_ref[0] ^ (flip ^ core), :, flip, c]
                     column_ref[c, at:at + pairs, flip, core * part:(core + 1) * part, :] = held
     full = column_ref[...].reshape(col_blocks * cols, width)
+    left = jnp.concatenate(
+        [gbar_ref[:, pl.ds(c, rows, stride=col_blocks), :] for c in range(col_blocks)], axis=2
+    )
+    product = dot(left.reshape(row_blocks * rows, col_blocks * cols), full)
     for b in range(row_blocks):
-        left = jnp.concatenate(
-            [gbar_ref[b, pl.ds(c, rows, stride=col_blocks), :] for c in range(col_blocks)], axis=1
-        )
-        out_ref[:, b * share:(b + 1) * share, :] = dot(left, full).reshape(n_col, share, width)
+        block = product[b * rows:(b + 1) * rows]
+        out_ref[:, b * share:(b + 1) * share, :] = block.reshape(n_col, share, width)
     ratio = col_blocks // row_blocks
     for b in range(row_blocks):
         local = column_ref[b * ratio + parity_ref[0]].reshape(n_col, share, width)

time: 113 us -> 113 us (level)
  no operation moved by 1% of the time
where the time goes in v11:
time: 113 us
  blocking collectives  90.1 us (80%)
  starting transfers between devices  11.5 us (10%)
  Pallas kernels  9.02 us (8%)
  waiting for transfers between devices  1.73 us (2%)
    all_gather x1, blocking collectives, per_device(): lax.all_gather(panel, ('z', 'core'), axis=0, axis_index_groups=rings, til...  36.7 us
    all_to_all x1, blocking collectives, per_device(): got = lax.all_to_all(sent, 'col', 0, 0, tiled=True)  20.7 us
    all_to_all x1, blocking collectives, per_device(): stage = lax.all_to_all(stage, near, 0, 0, tiled=True).reshape(width, width)  13.9 us
    all_to_all x1, blocking collectives, per_device(): slices = lax.all_to_all(corner, near, 0, 0, tiled=True)  11.6 us
    all_to_all x1, starting transfers between devices, per_device(): lax.all_to_all(folded, ('z', 'core'), 0, 0, tiled=True, axis_index_groups...  11.5 us
    pallas_call x8, Pallas kernels, call(): pl.pallas_call(kernel, out_shape=jax.tree.map(lambda s: jax.ShapeDtypeStr...  9.02 us
    all_gather x1, blocking collectives, per_device(): lax.all_gather(halves, 'core', axis=0)  2.78 us
  transfers between devices with their start and end apart: 1, of which 1 were waited for; matrix products, arithmetic and copies ran while one was open for 0% of the time, Pallas kernels for 4%

profile of v11, /device:TPU:1, one launch (start us, length us, event | category | flops | bytes accessed | tf_op | source)
XLA Modules:
  0.0 113.1 jit_solution(12565011805302040825)
XLA Ops:
  0.6 0.0 copy-start.1
  0.7 36.7 %all_gather.15 = f32[128,4,256]{2,1,0:T(4,128)S(1)} all-gather(f32[8,4,256]{2,1,0:T(4,128)} %param.6), channel_id=1, replica_groups={{0,48,64,112,128,176,192,240,256,304,320,368,384,432,448,496},{16,32,80..., dimensions={0}, use_global_device_ids=true | all-gather | bytes 557056 | tf_op jit(solution)/shard_map/all_gather | solution.py:145
  37.4 2.2 %all_gather.16 = f32[128,4,256]{2,1,0:T(4,128)S(1)} all-gather(f32[64,4,256]{2,1,0:T(4,128)S(1)} %get-tuple-element.32), channel_id=1, replica_groups=mesh['z'=16,'core'=2,'col'=16] {'core'}, dimensions={0}, use_global_device_ids=true | all-gather | bytes 786432 | tf_op jit(solution)/shard_map/all_gather | solution.py:147
  39.6 2.2 %all_gather.17 = f32[128,4,256]{2,1,0:T(4,128)S(1)} all-gather(f32[64,4,256]{2,1,0:T(4,128)S(1)} %get-tuple-element.18), channel_id=1, replica_groups=mesh['z'=16,'core'=2,'col'=16] {'core'}, dimensions={0}, use_global_device_ids=true | all-gather | bytes 786432 | tf_op jit(solution)/shard_map/all_gather | solution.py:149
  41.7 0.0 copy-done.1
  41.7 0.0 copy-start
  41.7 2.3 %shard_map.68 = f32[16,48,256]{2,1,0:T(8,128)S(1)} custom-call(s32[1]{0:T(128)} %bitcast.3.parity_ref, s32[1]{0:T(128)} %bitcast.4.turn_ref, s32[1]{0:T(128)} %bitcast.1.core_ref, f32[4,1024,128]{2,1,0:T(8,128)S(1)} %bitcast.17, f32[2,4,2,8,4,256]{5,4,3,2,1,0:T(4,128)S(1)} %bitcast.13, f32[2,4,2,8,4,256]{5,4,3,2,1,0:T(4,128)S(1)} %bitcast.14), custom_call_target="tpu_custom_call" | custom-call | flops 1600000000 | bytes 4194304 | tf_op jit(solution)/shard_map/pallas_call | solution.py:28
  44.1 0.0 copy-start.2
  44.1 0.0 copy-start.3
  44.1 20.7 %all_to_all.20.got_ref = f32[16,48,256]{2,1,0:T(8,128)S(1)} all-to-all(f32[16,48,256]{2,1,0:T(8,128)S(1)} %shard_map.68), channel_id=1, replica_groups=mesh['z'=16,'core'=2,'col'=16] {'col'}, dimensions={0} | all-to-all | bytes 1572864 | tf_op jit(solution)/shard_map/all_to_all | solution.py:166
  64.8 0.0 copy-done
  64.8 2.8 %all-gather = f32[4,16,256]{2,1,0:T(8,128)S(1)} all-gather(f32[2,16,256]{2,1,0:T(8,128)S(1)} %get-tuple-element.24), channel_id=2, replica_groups=mesh['z'=16,'core'=2,'col'=16] {'core'}, dimensions={0}, use_global_device_ids=true | all-gather | bytes 98304 | tf_op jit(solution)/shard_map/all_gather | solution.py:179
  67.6 0.4 shard_map.70
  68.0 11.6 %all_to_all.21.parts_ref = f32[32,8,256]{2,1,0:T(8,128)S(1)} all-to-all(f32[32,8,256]{2,1,0:T(8,128)S(1)} %shard_map.70), channel_id=1, replica_groups=mesh['z'=16,'core'=2,'col'=16] {'core','col'}, dimensions={0} | all-to-all | bytes 524288 | tf_op jit(solution)/shard_map/all_to_all | solution.py:184
  79.6 0.7 shard_map.71
  80.3 11.5 %all-to-all-start.2 = ((f32[16,8,256]{2,1,0:T(8,128)}), f32[16,8,256]{2,1,0:T(8,128)S(1)}, u32[]{:S(2)}, u32[]{:S(2)}) async-start(f32[16,8,256]{2,1,0:T(8,128)} %shard_map.71), calls=%async_computation.2 | async-start | bytes 262144 | tf_op jit(solution)/shard_map/all_to_all | solution.py:189
  91.8 0.0 copy-done.2
  91.8 0.0 copy-done.3
  91.8 3.3 %shard_map.72 = (f32[256,256]{1,0:T(8,128)S(1)}, f32[256,256]{1,0:T(8,128)S(1)}) custom-call(f32[256,256]{1,0:T(8,128)S(1)} %copy-done.2, f32[256,256]{1,0:T(8,128)S(1)} %copy-done.3), custom_call_target="tpu_custom_call" | custom-call | flops 3200000000 | bytes 524288 | tf_op jit(solution)/shard_map/pallas_call | solution.py:28
  95.1 0.8 shard_map.73
  96.0 1.7 %all-to-all-done.2.parts_ref = f32[16,8,256]{2,1,0:T(8,128)S(1)} async-done(((f32[16,8,256]{2,1,0:T(8,128)}), f32[16,8,256]{2,1,0:T(8,128)S(1)}, u32[]{:S(2)}, u32[]{:S(2)}) %all-to-all-start.2) | async-done | bytes 131104 | tf_op jit(solution)/shard_map/all_to_all | solution.py:189
  97.7 0.2 shard_map.74
  97.9 13.9 %all_to_all.22 = f32[32,8,256]{2,1,0:T(8,128)S(1)} all-to-all(f32[32,8,256]{2,1,0:T(8,128)S(1)} %shard_map.74), channel_id=1, replica_groups=mesh['z'=16,'core'=2,'col'=16] {'core','col'}, dimensions={0} | all-to-all | bytes 524288 | tf_op jit(solution)/shard_map/all_to_all | solution.py:214
  111.9 1.2 %shard_map.75 = f32[256,256]{1,0:T(8,128)} custom-call(f32[256,256]{1,0:T(8,128)S(1)} %bitcast.12, f32[256,256]{1,0:T(8,128)S(1)} %get-tuple-element.28.inverse_ref), custom_call_target="tpu_custom_call" | custom-call | tf_op jit(solution)/shard_map/pallas_call | solution.py:28
  (2 shorter events, 0.1 us)
Async XLA Ops:
  0.6 41.1 %copy-start.1 = (f32[4,128,8,128]{3,2,1,0:T(8,128)S(1)}, f32[4,128,8,128]{3,2,1,0:T(8,128)}, u32[]{:S(2)}) copy-start(f32[4,128,8,128]{3,2,1,0:T(8,128)} %param.5) | copy-start | bytes 6291460
  41.7 23.0 %copy-start = (f32[4,8,256]{2,1,0:T(8,128)S(1)}, f32[4,8,256]{2,1,0:T(8,128)}, u32[]{:S(2)}) copy-start(f32[4,8,256]{2,1,0:T(8,128)} %param.7) | copy-start | bytes 98308
  44.1 47.8 %copy-start.2 = (f32[256,256]{1,0:T(8,128)S(1)}, f32[256,256]{1,0:T(8,128)}, u32[]{:S(2)}) copy-start(f32[256,256]{1,0:T(8,128)} %factor_ref) | copy-start | bytes 786436
  44.1 47.8 %copy-start.3 = (f32[256,256]{1,0:T(8,128)S(1)}, f32[256,256]{1,0:T(8,128)}, u32[]{:S(2)}) copy-start(f32[256,256]{1,0:T(8,128)} %adjoint_ref.1) | copy-start | bytes 786436
  80.3 17.3 %all-to-all-start.2 = ((f32[16,8,256]{2,1,0:T(8,128)}), f32[16,8,256]{2,1,0:T(8,128)S(1)}, u32[]{:S(2)}, u32[]{:S(2)}) async-start(f32[16,8,256]{2,1,0:T(8,128)} %shard_map.71), calls=%async_computation.2 | async-start | bytes 262144 | tf_op jit(solution)/shard_map/all_to_all | solution.py:189

commit v12 on v9

--- a/solution.py
+++ b/solution.py
@@ -92,14 +92,19 @@
         halves_ref[core] = got_ref[source_ref[0] + core, owned:, :]
 
 
-def corner_kernel(part, core_ref, halves_ref, total_ref, corner_ref, mine_ref):
+def corner_kernel(part, core_ref, turn_ref, halves_ref, total_ref, corner_ref, mine_ref):
     n_core, _, half, _ = halves_ref.shape
     for core in range(n_core):
         rows = halves_ref[core, core_ref[0]]
         for b in range(half // part):
             at = (b * n_core + core) * part
             mine_ref[at:at + part, :] = rows[b * part:(b + 1) * part]
-    corner_ref[...] = dot_tn(mine_ref[...], total_ref[...]).reshape(corner_ref.shape)
+    corner = dot_tn(mine_ref[...], total_ref[...])
+    n_col = corner_ref.shape[0] // n_core
+    for core in range(n_core):
+        held = corner[core * n_col * corner_ref.shape[1]:(core + 1) * n_col * corner_ref.shape[1]]
+        at = (turn_ref[0] ^ core) * n_col
+        corner_ref[pl.ds(at, n_col)] = held.reshape(n_col, *corner_ref.shape[1:])
 
 
 def lower_kernel(total_ref, inverse_ref, out_ref):
@@ -122,8 +127,9 @@
     out_ref[...] = jnp.broadcast_to(stage[None], out_ref.shape)
 
 
-def finish_kernel(stage_ref, inverse_ref, out_ref):
-    middle = dot_tn(inverse_ref[...], stage_ref[...])
+def finish_kernel(turn_ref, stage_ref, inverse_ref, out_ref):
+    stage = jnp.concatenate([stage_ref[turn_ref[0] ^ core] for core in range(2)], axis=0)
+    middle = dot_tn(inverse_ref[...], stage)
     out_ref[...] = 0.5 * (middle + middle.T)
 
 
@@ -147,13 +153,14 @@
     both = [first, lax.all_gather(rest, "core", axis=0, tiled=True)]
     source = (lax.axis_index("z") * n_core % n_col)[None]
     core_here = core_at[None]
+    turn = (lax.axis_index("z") % 2)[None]
     adjoint = panel_adj.reshape(row_blocks * share, width)
-    *both, source, core_here, adjoint = lax.optimization_barrier((*both, source, core_here, adjoint))
+    *both, source, core_here, turn, adjoint = lax.optimization_barrier((*both, source, core_here, turn, adjoint))
     sent = call(
         product_kernel,
         (n_col, row_blocks * (share + part), width),
         (row_at // n_col)[None],
-        (lax.axis_index("z") % 2)[None],
+        turn,
         core_here,
         gbar.reshape(row_blocks, rows * col_blocks, cols),
         *[b.reshape(n_core, n_z // 4, 2, col_blocks, part, width) for b in both],
@@ -174,16 +181,17 @@
         functools.partial(corner_kernel, part),
         (n_near, count, width),
         core_here,
+        turn,
         lax.all_gather(halves, "core", axis=0),
         total,
         scratch=[pltpu.VMEM((row_blocks * share, width), F32)],
-        scalars=1,
+        scalars=2,
     )
     slices = lax.all_to_all(corner, near, 0, 0, tiled=True)
     folded, factor = lax.optimization_barrier(
         (call(fold_kernel, (n_z, count, width), slices), factor)
     )
-    lines = [[(z + n_z // 2) % n_z * n_core + core for z in range(n_z)] for core in range(n_core)]
+    lines = [ring[n_z // 2:] + ring[:n_z // 2] for ring in rings]
     piece = lax.all_to_all(folded, ("z", "core"), 0, 0, tiled=True, axis_index_groups=lines)
     inverse, known = call(
         invert_kernel,
@@ -203,14 +211,15 @@
     stage = call(
         slice_kernel,
         (n_near, count, width),
-        ((core_at * n_col + col_at) * count)[None],
+        (((core_at ^ turn[0]) * n_col + col_at) * count)[None],
         piece,
         known,
         inverse,
         scalars=1,
     )
-    stage = lax.all_to_all(stage, near, 0, 0, tiled=True).reshape(width, width)
-    corner_adj = call(finish_kernel, (width, width), stage, inverse)
+    stage = lax.all_to_all(stage, near, 0, 0, tiled=True)
+    stage = stage.reshape(n_core, width // n_core, width)
+    corner_adj = call(finish_kernel, (width, width), turn, stage, inverse, scalars=1)
     return lower.reshape(row_blocks, share, width), corner_adj
 
 

time: 113 us -> 113 us (level)
  waiting for transfers between devices: 1.73 us -> 3.11 us
  blocking collectives: 90.1 us -> 88.8 us
    all_to_all x1, waiting for transfers between devices: 1.73 us -> 3.11 us  [per_device(): lax.all_to_all(folded, ('z', 'core'), 0, 0, tiled=True, axis_index_groups...]
    all_to_all x1, blocking collectives: 13.9 us -> 12.6 us  [per_device(): stage = lax.all_to_all(stage, near, 0, 0, tiled=True)]
where the time goes in v12:
time: 113 us
  blocking collectives  88.8 us (79%)
  starting transfers between devices  11.5 us (10%)
  Pallas kernels  8.92 us (8%)
  waiting for transfers between devices  3.11 us (3%)
    all_gather x1, blocking collectives, per_device(): lax.all_gather(panel, ('z', 'core'), axis=0, axis_index_groups=rings, til...  36.7 us
    all_to_all x1, blocking collectives, per_device(): got = lax.all_to_all(sent, 'col', 0, 0, tiled=True)  20.7 us
    all_to_all x1, blocking collectives, per_device(): stage = lax.all_to_all(stage, near, 0, 0, tiled=True)  12.6 us
    all_to_all x1, blocking collectives, per_device(): slices = lax.all_to_all(corner, near, 0, 0, tiled=True)  11.6 us
    all_to_all x1, starting transfers between devices, per_device(): lax.all_to_all(folded, ('z', 'core'), 0, 0, tiled=True, axis_index_groups...  11.5 us
    pallas_call x8, Pallas kernels, call(): pl.pallas_call(kernel, out_shape=jax.tree.map(lambda s: jax.ShapeDtypeStr...  8.92 us
    all_to_all x1, waiting for transfers between devices, per_device(): lax.all_to_all(folded, ('z', 'core'), 0, 0, tiled=True, axis_index_groups...  3.11 us
    all_gather x1, blocking collectives, per_device(): lax.all_gather(halves, 'core', axis=0)  2.77 us
  transfers between devices with their start and end apart: 1, of which 1 were waited for; matrix products, arithmetic and copies ran while one was open for 0% of the time, Pallas kernels for 4%

profile of v12, /device:TPU:1, one launch (start us, length us, event | category | flops | bytes accessed | tf_op | source)
XLA Modules:
  0.0 113.0 jit_solution(18346220690676522664)
XLA Ops:
  0.6 0.0 copy-start.1
  0.7 36.7 %all_gather.15 = f32[128,4,256]{2,1,0:T(4,128)S(1)} all-gather(f32[8,4,256]{2,1,0:T(4,128)} %param.6), channel_id=1, replica_groups={{0,48,64,112,128,176,192,240,256,304,320,368,384,432,448,496},{16,32,80..., dimensions={0}, use_global_device_ids=true | all-gather | bytes 557056 | tf_op jit(solution)/shard_map/all_gather | solution.py:149
  37.4 2.2 %all_gather.16 = f32[128,4,256]{2,1,0:T(4,128)S(1)} all-gather(f32[64,4,256]{2,1,0:T(4,128)S(1)} %get-tuple-element.34), channel_id=1, replica_groups=mesh['z'=16,'core'=2,'col'=16] {'core'}, dimensions={0}, use_global_device_ids=true | all-gather | bytes 786432 | tf_op jit(solution)/shard_map/all_gather | solution.py:151
  39.6 2.2 %all_gather.17 = f32[128,4,256]{2,1,0:T(4,128)S(1)} all-gather(f32[64,4,256]{2,1,0:T(4,128)S(1)} %get-tuple-element.19), channel_id=1, replica_groups=mesh['z'=16,'core'=2,'col'=16] {'core'}, dimensions={0}, use_global_device_ids=true | all-gather | bytes 786432 | tf_op jit(solution)/shard_map/all_gather | solution.py:153
  41.7 0.0 copy-done.1
  41.7 0.0 copy-start
  41.7 2.2 %shard_map.68 = f32[16,48,256]{2,1,0:T(8,128)S(1)} custom-call(s32[1]{0:T(128)} %bitcast.4.parity_ref, s32[1]{0:T(128)} %bitcast.2.turn_ref, s32[1]{0:T(128)} %bitcast.1.core_ref, f32[4,1024,128]{2,1,0:T(8,128)S(1)} %bitcast.18, f32[2,4,2,8,4,256]{5,4,3,2,1,0:T(4,128)S(1)} %bitcast.14, f32[2,4,2,8,4,256]{5,4,3,2,1,0:T(4,128)S(1)} %bitcast.15), custom_call_target="tpu_custom_call" | custom-call | flops 1600000000 | bytes 4194304 | tf_op jit(solution)/shard_map/pallas_call | solution.py:28
  43.9 0.0 copy-start.2
  44.0 0.0 copy-start.3
  44.0 20.7 %all_to_all.20.got_ref = f32[16,48,256]{2,1,0:T(8,128)S(1)} all-to-all(f32[16,48,256]{2,1,0:T(8,128)S(1)} %shard_map.68), channel_id=1, replica_groups=mesh['z'=16,'core'=2,'col'=16] {'col'}, dimensions={0} | all-to-all | bytes 1572864 | tf_op jit(solution)/shard_map/all_to_all | solution.py:171
  64.7 0.0 copy-done
  64.7 2.8 %all-gather = f32[4,16,256]{2,1,0:T(8,128)S(1)} all-gather(f32[2,16,256]{2,1,0:T(8,128)S(1)} %get-tuple-element.26), channel_id=2, replica_groups=mesh['z'=16,'core'=2,'col'=16] {'core'}, dimensions={0}, use_global_device_ids=true | all-gather | bytes 98304 | tf_op jit(solution)/shard_map/all_gather | solution.py:185
  67.5 0.4 shard_map.70
  67.9 11.6 %all_to_all.21.parts_ref = f32[32,8,256]{2,1,0:T(8,128)S(1)} all-to-all(f32[32,8,256]{2,1,0:T(8,128)S(1)} %shard_map.70), channel_id=1, replica_groups=mesh['z'=16,'core'=2,'col'=16] {'core','col'}, dimensions={0} | all-to-all | bytes 524288 | tf_op jit(solution)/shard_map/all_to_all | solution.py:190
  79.5 0.7 shard_map.71
  80.2 11.5 %all-to-all-start.2 = ((f32[16,8,256]{2,1,0:T(8,128)}), f32[16,8,256]{2,1,0:T(8,128)S(1)}, u32[]{:S(2)}, u32[]{:S(2)}) async-start(f32[16,8,256]{2,1,0:T(8,128)} %shard_map.71), calls=%async_computation.2 | async-start | bytes 262144 | tf_op jit(solution)/shard_map/all_to_all | solution.py:195
  91.7 0.0 copy-done.2
  91.7 0.0 copy-done.3
  91.7 3.3 %shard_map.72 = (f32[256,256]{1,0:T(8,128)S(1)}, f32[256,256]{1,0:T(8,128)S(1)}) custom-call(f32[256,256]{1,0:T(8,128)S(1)} %copy-done.2, f32[256,256]{1,0:T(8,128)S(1)} %copy-done.3), custom_call_target="tpu_custom_call" | custom-call | flops 3200000000 | bytes 524288 | tf_op jit(solution)/shard_map/pallas_call | solution.py:28
  95.0 0.8 shard_map.73
  95.9 3.1 %all-to-all-done.2.parts_ref = f32[16,8,256]{2,1,0:T(8,128)S(1)} async-done(((f32[16,8,256]{2,1,0:T(8,128)}), f32[16,8,256]{2,1,0:T(8,128)S(1)}, u32[]{:S(2)}, u32[]{:S(2)}) %all-to-all-start.2) | async-done | bytes 131104 | tf_op jit(solution)/shard_map/all_to_all | solution.py:195
  99.0 0.2 shard_map.74
  99.2 12.6 %all_to_all.22 = f32[32,8,256]{2,1,0:T(8,128)S(1)} all-to-all(f32[32,8,256]{2,1,0:T(8,128)S(1)} %shard_map.74), channel_id=1, replica_groups=mesh['z'=16,'core'=2,'col'=16] {'core','col'}, dimensions={0} | all-to-all | bytes 524288 | tf_op jit(solution)/shard_map/all_to_all | solution.py:220
  111.8 1.2 %shard_map.75 = f32[256,256]{1,0:T(8,128)} custom-call(s32[1]{0:T(128)} %bitcast.2.turn_ref, f32[2,128,256]{2,1,0:T(8,128)S(1)} %bitcast.13, f32[256,256]{1,0:T(8,128)S(1)} %get-tuple-element.30.inverse_ref), custom_call_target="tpu_custom_call" | custom-call | tf_op jit(solution)/shard_map/pallas_call | solution.py:28
  (2 shorter events, 0.1 us)
Async XLA Ops:
  0.6 41.1 %copy-start.1 = (f32[4,128,8,128]{3,2,1,0:T(8,128)S(1)}, f32[4,128,8,128]{3,2,1,0:T(8,128)}, u32[]{:S(2)}) copy-start(f32[4,128,8,128]{3,2,1,0:T(8,128)} %param.5) | copy-start | bytes 6291460
  41.7 23.0 %copy-start = (f32[4,8,256]{2,1,0:T(8,128)S(1)}, f32[4,8,256]{2,1,0:T(8,128)}, u32[]{:S(2)}) copy-start(f32[4,8,256]{2,1,0:T(8,128)} %param.7) | copy-start | bytes 98308
  43.9 47.8 %copy-start.2 = (f32[256,256]{1,0:T(8,128)S(1)}, f32[256,256]{1,0:T(8,128)}, u32[]{:S(2)}) copy-start(f32[256,256]{1,0:T(8,128)} %factor_ref) | copy-start | bytes 786436
  44.0 47.8 %copy-start.3 = (f32[256,256]{1,0:T(8,128)S(1)}, f32[256,256]{1,0:T(8,128)}, u32[]{:S(2)}) copy-start(f32[256,256]{1,0:T(8,128)} %adjoint_ref.1) | copy-start | bytes 786436
  80.2 18.7 %all-to-all-start.2 = ((f32[16,8,256]{2,1,0:T(8,128)}), f32[16,8,256]{2,1,0:T(8,128)S(1)}, u32[]{:S(2)}, u32[]{:S(2)}) async-start(f32[16,8,256]{2,1,0:T(8,128)} %shard_map.71), calls=%async_computation.2 | async-start | bytes 262144 | tf_op jit(solution)/shard_map/all_to_all | solution.py:195
